TPU v7x, 512 devices: a whole 4x8x8 slice. The times are simulated.
512 devices in a mesh: frame: 16 (over z, core), height: 32 (over x, y).
Axes of the slice: x: 4, y: 8, z: 8, core: 2. Of those that a mesh axis runs over, the one named last changes fastest.
Arguments:
- video: bfloat16 [33, 64, 128, 256], P(None, 'height', 'frame'), may hold values from -48 to 48
- frame_counts: int32 [16], replicated, may hold values from 1 to 6, 33 in all
- temporal_weight: bfloat16 [6912, 256], replicated, may hold values from -0.125 to 0.125
- temporal_bias: float32 [256], replicated, may hold values from -4 to 4
- first_gain: float32 [256], replicated, may hold values from 0.1 to 1.9
- first_shift: float32 [256], replicated, may hold values from -3 to 3
- first_weight: bfloat16 [2304, 256], P('height'), may hold values from -0.125 to 0.125
- first_bias: float32 [256], replicated, may hold values from -4 to 4
- second_gain: float32 [256], replicated, may hold values from 0.1 to 1.9
- second_shift: float32 [256], replicated, may hold values from -3 to 3
- second_weight: bfloat16 [2304, 256], P('height'), may hold values from -0.125 to 0.125
- second_bias: float32 [256], replicated, may hold values from -4 to 4
Outputs:
- owned: bfloat16 [96, 64, 128, 256], P('frame', 'height')
Inputs may be any that keep to these rules, and one draw needn't show every extreme that they name: frame_counts[k] consecutive frames belong to index k of frame; the counts add up to 33 and the largest is exactly 6.
All inputs are finite; a program needn't handle non-finite values.
Results may differ from a plain program's by a relative error of at most 0.0055.
Values may be sent and summed in bfloat16 or wider, within the bound.
A program may use at most 64 MiB of HBM per device.

v0:
```python
import jax
import jax.numpy as jnp
from jax import lax
from jax.sharding import PartitionSpec as P

GROUPS = 32


def with_halo(array, sides, width):
    for axis, dim in sides:
        size, length = (lax.axis_size(axis), array.shape[dim])
        up = [(i, (i + 1) % size) for i in range(size - 1)]
        down = [(j, i) for i, j in up]
        last = lax.slice_in_dim(array, length - width, length, axis=dim)
        first = lax.slice_in_dim(array, 0, width, axis=dim)
        before = lax.ppermute(last, axis, up)
        after = lax.ppermute(first, axis, down)
        array = jnp.concatenate([before, array, after], axis=dim)
    return array


def spatial_patches(padded, row_count, col_count):
    pieces = []
    for row_tap in range(3):
        for col_tap in range(3):
            pieces.append(
                padded[:, row_tap : row_tap + row_count, col_tap : col_tap + col_count, :]
            )
    return jnp.concatenate(pieces, axis=-1)


def group_act(tensor, gain_row, shift_row, totals, cell_count):
    frame_slots, row_count, col_count, channels = tensor.shape
    width_group = channels // GROUPS
    grouped = tensor.astype(jnp.float32).reshape(
        frame_slots, row_count, col_count, GROUPS, width_group
    )
    part_sum = jnp.sum(grouped, axis=(1, 2, 4))
    part_sq = jnp.sum(grouped * grouped, axis=(1, 2, 4))
    total_sum, total_sq = totals(part_sum, part_sq)
    sample = float(cell_count * width_group)
    group_mean = total_sum / sample
    group_var = total_sq / sample - group_mean * group_mean
    inverse = lax.rsqrt(group_var + 1e-06)
    normed = (grouped - group_mean[:, None, None, :, None]) * inverse[:, None, None, :, None]
    normed = normed.reshape(frame_slots, row_count, col_count, channels) * gain_row + shift_row
    return jax.nn.silu(normed).astype(jnp.bfloat16)


def convolve(padded, weight_shard, offset_bias):
    frame_slots, row_span, col_span, channels = padded.shape
    row_count = row_span - 2
    col_count = col_span - 2
    patches = spatial_patches(padded, row_count, col_count).reshape(
        frame_slots * row_count * col_count, 9 * channels
    )
    accumulated = jnp.dot(
        patches,
        lax.all_gather(weight_shard, "height", axis=0, tiled=True),
        preferred_element_type=jnp.float32,
    )
    return (accumulated + offset_bias).reshape(frame_slots, row_count, col_count, channels)


def resnet(
    tensor,
    extend,
    totals,
    cell_count,
    first_gain,
    first_shift,
    first_weight,
    first_bias,
    second_gain,
    second_shift,
    second_weight,
    second_bias,
):
    first_in = group_act(tensor, first_gain, first_shift, totals, cell_count)
    first_out = convolve(extend(first_in), first_weight, first_bias).astype(jnp.bfloat16)
    second_in = group_act(first_out, second_gain, second_shift, totals, cell_count)
    return (
        tensor.astype(jnp.float32) + convolve(extend(second_in), second_weight, second_bias)
    ).astype(jnp.bfloat16)


def per_device(
    video,
    frame_counts,
    temporal_weight,
    temporal_bias,
    first_gain,
    first_shift,
    first_weight,
    first_bias,
    second_gain,
    second_shift,
    second_weight,
    second_bias,
):
    frames, row_count, col_count, channels = video.shape
    n_frame = lax.axis_size("frame")
    n_height = lax.axis_size("height")
    capacity = min(2 * ((frames + n_frame - 1) // n_frame), frames - n_frame + 1)
    activated = jax.nn.silu(video.astype(jnp.float32)).astype(jnp.bfloat16)
    bordered = with_halo(activated, (("frame", 2), ("height", 1)), 1)
    causal = jnp.pad(bordered, ((2, 0), (0, 0), (0, 0), (0, 0)))
    accumulated = jnp.zeros((frames * row_count * col_count, channels), jnp.float32)
    for tap_time in range(3):
        patches = spatial_patches(causal[tap_time : tap_time + frames], row_count, col_count)
        patches = patches.reshape(frames * row_count * col_count, 9 * channels)
        accumulated = accumulated + jnp.dot(
            patches,
            temporal_weight[tap_time * 9 * channels : (tap_time + 1) * 9 * channels],
            preferred_element_type=jnp.float32,
        )
    blended = (video.astype(jnp.float32) + accumulated.reshape(video.shape) + temporal_bias).astype(
        jnp.bfloat16
    )
    offsets = jnp.cumsum(frame_counts) - frame_counts
    peer_ids = jnp.arange(n_frame, dtype=jnp.int32)
    cell_count = row_count * n_height * col_count * n_frame

    def extend(tensor):
        extended = with_halo(tensor, (("height", 1),), 1)
        return jnp.pad(extended, ((0, 0), (0, 0), (1, 1), (0, 0)))

    def totals(part_sum, part_sq):
        return lax.psum((part_sum, part_sq), "height")

    slot_ids = jnp.arange(n_frame * capacity, dtype=jnp.int32)
    owner_idx = slot_ids // capacity
    within = slot_ids - owner_idx * capacity
    matches = owner_idx[:, None] == peer_ids[None, :]
    first_frame = jnp.sum(jnp.where(matches, offsets[None, :], 0), axis=1)
    frame_total = jnp.sum(jnp.where(matches, frame_counts[None, :], 0), axis=1)
    source_idx = jnp.clip(first_frame + within, 0, frames - 1)
    picked = jnp.take(blended, source_idx, axis=0)
    retained = jnp.where(
        (within < frame_total)[:, None, None, None], picked, jnp.zeros_like(picked)
    )
    owned_frames = lax.all_to_all(retained, "frame", split_axis=0, concat_axis=2, tiled=True)
    decoded = resnet(
        owned_frames,
        extend,
        totals,
        cell_count,
        first_gain,
        first_shift,
        first_weight,
        first_bias,
        second_gain,
        second_shift,
        second_weight,
        second_bias,
    )
    my_count = jnp.sum(jnp.where(peer_ids == lax.axis_index("frame"), frame_counts, 0))
    live_slots = jnp.arange(capacity, dtype=jnp.int32) < my_count
    return jnp.where(live_slots[:, None, None, None], decoded, jnp.zeros_like(decoded))


def solution(mesh):
    placed = (
        P(None, "height", "frame", None),
        P(),
        P(),
        P(),
        P(),
        P(),
        P("height", None),
        P(),
        P(),
        P(),
        P("height", None),
        P(),
    )
    return jax.shard_map(
        per_device,
        mesh=mesh,
        in_specs=placed,
        out_specs=P("frame", "height", None, None),
        check_vma=False,
    )
```

profile of v0, /device:TPU:1, one launch (start us, length us, event | category | flops | bytes accessed | tf_op | source)
XLA Modules:
  0.0 404.1 jit_solution(1805875194880069992)
XLA Ops:
  7.8 5.4 %collective-permute-start = (bf16[33,2,1,256]{3,2,1,0:T(2,128)(2,1)S(1)}, bf16[33,2,1,256]{3,2,1,0:T(2,128)(2,1)S(1)}, u32[]{:S(2)}, u32[]{:S(2)}) collective-permute-start(bf16[33,2,1,256]{3,2,1,0:T(2,128)(2,1)S(1)} %get-tuple-element.41), channel_id=1, source_target_pairs={{0,32},{32,64},{64,96},{96,128},{128,160},{160,192},{192,224},{224... | collective-permute-start | bytes 101384 | tf_op jit(solution)/shard_map/ppermute | solution.py:16
  13.1 4.7 %collective-permute-start.1 = (bf16[33,2,1,256]{3,2,1,0:T(2,128)(2,1)S(1)}, bf16[33,2,1,256]{3,2,1,0:T(2,128)(2,1)S(1)}, u32[]{:S(2)}, u32[]{:S(2)}) collective-permute-start(bf16[33,2,1,256]{3,2,1,0:T(2,128)(2,1)S(1)} %get-tuple-element.42), channel_id=1, source_target_pairs={{32,0},{64,32},{96,64},{128,96},{160,128},{192,160},{224,192},{256... | collective-permute-start | bytes 101384 | tf_op jit(solution)/shard_map/ppermute | solution.py:17
  23.9 4.5 %collective-permute-done.2 = bf16[33,1,10,256]{3,2,1,0:T(8,128)(2,1)S(1)} collective-permute-done((bf16[33,1,10,256]{3,2,1,0:T(8,128)(2,1)S(1)}, bf16[33,1,10,256]{3,2,1,0:T(8,128)(2,1)S(1)}, u32[]{:S(2)}, u32[]{:S(2)}) %collective-permute-start.2) | collective-permute-done | bytes 168992 | tf_op jit(solution)/shard_map/ppermute | solution.py:16
  28.4 4.2 %collective-permute-done.3 = bf16[33,1,10,256]{3,2,1,0:T(8,128)(2,1)S(1)} collective-permute-done((bf16[33,1,10,256]{3,2,1,0:T(8,128)(2,1)S(1)}, bf16[33,1,10,256]{3,2,1,0:T(8,128)(2,1)S(1)}, u32[]{:S(2)}, u32[]{:S(2)}) %collective-permute-start.3) | collective-permute-done | bytes 168992 | tf_op jit(solution)/shard_map/ppermute | solution.py:17
  35.6 1.7 copy-done.9
  40.8 32.5 %all_to_all.4 = bf16[96,2,8,256]{3,2,1,0:T(8,128)(2,1)S(1)} all-to-all(bf16[96,2,8,256]{3,2,1,0:T(8,128)(2,1)S(1)} %select_select_fusion), channel_id=1, replica_groups=mesh['frame'=16,'height'=32] {'frame'}, dimensions={0} | all-to-all | bytes 1572864 | tf_op jit(solution)/shard_map/all_to_all | solution.py:142
  73.9 60.6 %all-reduce.4 = (f32[6,32]{1,0:T(8,128)S(1)}, f32[6,32]{1,0:T(8,128)S(1)}) all-reduce(f32[6,32]{1,0:T(8,128)S(1)} %reduce_sum.88, f32[6,32]{1,0:T(8,128)S(1)} %reduce_sum.85), channel_id=1, replica_groups=mesh['frame'=16,'height'=32] {'height'}, use_global_device_ids=true, to_apply=%region_9.10 | all-reduce | flops 384 | bytes 3072 | tf_op jit(solution)/shard_map/psum | solution.py:129
  138.4 3.2 collective-permute-done.4
  141.6 4.0 %collective-permute-done.5 = bf16[6,1,128,256]{3,2,1,0:T(8,128)(2,1)S(1)} collective-permute-done((bf16[6,1,128,256]{3,2,1,0:T(8,128)(2,1)S(1)}, bf16[6,1,128,256]{3,2,1,0:T(8,128)(2,1)S(1)}, u32[]{:S(2)}, u32[]{:S(2)}) %collective-permute-start.5) | collective-permute-done | bytes 393248 | tf_op jit(solution)/shard_map/ppermute | solution.py:17
  150.8 1.5 constant_dynamic-update-slice_fusion.1
  156.7 63.7 %all-gather.3.cloned.1.call-done = bf16[2304,256]{1,0:T(8,128)(2,1)} async-done(((bf16[72,256]{1,0:T(8,128)(2,1)}), bf16[2304,256]{1,0:T(8,128)(2,1)}) %all-gather.3.cloned.1.call-update) | async-done | bytes 1179664 | tf_op jit(solution)/shard_map/all_gather | solution.py:59
  220.4 5.3 %fusion.2 = f32[1536,256]{1,0:T(8,128)S(1)} fusion(bf16[1536,2304]{1,0:T(8,128)(2,1)} %bitcast.11, bf16[2304,256]{1,0:T(8,128)(2,1)} %all-gather.3.cloned.1.call-done, f32[256]{0:T(256)S(1)} %copy-done.10), kind=kOutput, calls=%fused_computation.7 | convolution fusion | flops 1813118976 | bytes 9831424 | tf_op jit(solution)/shard_map/dot_general | solution.py:57
  225.7 1.6 copy.32
  227.3 3.1 reshape.191
  230.4 3.2 fusion.45
  233.8 59.3 %all-reduce.3 = (f32[6,32]{1,0:T(8,128)S(1)}, f32[6,32]{1,0:T(8,128)S(1)}) all-reduce(f32[6,32]{1,0:T(8,128)S(1)} %copy.34, f32[6,32]{1,0:T(8,128)S(1)} %copy.33), channel_id=1, replica_groups=mesh['frame'=16,'height'=32] {'height'}, use_global_device_ids=true, to_apply=%region_13.14 | all-reduce | flops 384 | bytes 3072 | tf_op jit(solution)/shard_map/psum | solution.py:129
  294.9 2.1 collective-permute-start.6
  297.0 1.5 collective-permute-start.7
  299.9 1.5 collective-permute-done.6
  301.3 4.8 %collective-permute-done.7 = bf16[6,1,128,256]{3,2,1,0:T(8,128)(2,1)S(1)} collective-permute-done((bf16[6,1,128,256]{3,2,1,0:T(8,128)(2,1)}, bf16[6,1,128,256]{3,2,1,0:T(8,128)(2,1)S(1)}, u32[]{:S(2)}, u32[]{:S(2)}) %collective-permute-start.7) | collective-permute-done | bytes 393248 | tf_op jit(solution)/shard_map/ppermute | solution.py:17
  306.1 1.9 select_maximum_fusion
  309.1 2.1 fusion.28
  319.2 71.5 %all-gather.5.cloned.1.call-done = bf16[2304,256]{1,0:T(8,128)(2,1)} async-done(((bf16[72,256]{1,0:T(8,128)(2,1)}), bf16[2304,256]{1,0:T(8,128)(2,1)}) %all-gather.5.cloned.1.call-update) | async-done | bytes 1179664 | tf_op jit(solution)/shard_map/all_gather | solution.py:59
  390.6 5.4 %convolution_add_fusion = f32[1536,256]{1,0:T(8,128)S(1)} fusion(bf16[1536,2304]{1,0:T(8,128)(2,1)} %bitcast.13, bf16[2304,256]{1,0:T(8,128)(2,1)} %all-gather.5.cloned.1.call-done, f32[256]{0:T(256)S(1)} %copy-done.11), kind=kOutput, calls=%fused_computation.4 | convolution fusion | flops 1812332544 | bytes 9831424 | tf_op jit(solution)/shard_map/dot_general | solution.py:57
  (112 shorter events, 41.1 us)
Async XLA Ops:
  6.5 213.9 %all-gather.3.cloned.1.call-start = ((), (), s32[]{:S(2)}) async-start(), calls=%async_computation.1 | async-start | bytes 1216512 | tf_op jit(solution)/shard_map/all_gather | solution.py:59
  7.8 13.1 %collective-permute-start = (bf16[33,2,1,256]{3,2,1,0:T(2,128)(2,1)S(1)}, bf16[33,2,1,256]{3,2,1,0:T(2,128)(2,1)S(1)}, u32[]{:S(2)}, u32[]{:S(2)}) collective-permute-start(bf16[33,2,1,256]{3,2,1,0:T(2,128)(2,1)S(1)} %get-tuple-element.41), channel_id=1, source_target_pairs={{0,32},{32,64},{64,96},{96,128},{128,160},{160,192},{192,224},{224... | collective-permute-start | bytes 101384 | tf_op jit(solution)/shard_map/ppermute | solution.py:16
  13.1 7.7 %collective-permute-start.1 = (bf16[33,2,1,256]{3,2,1,0:T(2,128)(2,1)S(1)}, bf16[33,2,1,256]{3,2,1,0:T(2,128)(2,1)S(1)}, u32[]{:S(2)}, u32[]{:S(2)}) collective-permute-start(bf16[33,2,1,256]{3,2,1,0:T(2,128)(2,1)S(1)} %get-tuple-element.42), channel_id=1, source_target_pairs={{32,0},{64,32},{96,64},{128,96},{160,128},{192,160},{224,192},{256... | collective-permute-start | bytes 101384 | tf_op jit(solution)/shard_map/ppermute | solution.py:17
  21.3 7.1 %collective-permute-start.2 = (bf16[33,1,10,256]{3,2,1,0:T(8,128)(2,1)S(1)}, bf16[33,1,10,256]{3,2,1,0:T(8,128)(2,1)S(1)}, u32[]{:S(2)}, u32[]{:S(2)}) collective-permute-start(bf16[33,1,10,256]{3,2,1,0:T(8,128)(2,1)S(1)} %get-tuple-element.37), channel_id=1, source_target_pairs={{0,1},{1,2},{2,3},{3,4},{4,5},{5,6},{6,7},{7,8},{8,9},{9,10},{10,1... | collective-permute-start | bytes 506888 | tf_op jit(solution)/shard_map/ppermute | solution.py:16
  22.6 10.1 %collective-permute-start.3 = (bf16[33,1,10,256]{3,2,1,0:T(8,128)(2,1)S(1)}, bf16[33,1,10,256]{3,2,1,0:T(8,128)(2,1)S(1)}, u32[]{:S(2)}, u32[]{:S(2)}) collective-permute-start(bf16[33,1,10,256]{3,2,1,0:T(8,128)(2,1)S(1)} %get-tuple-element.38), channel_id=1, source_target_pairs={{1,0},{2,1},{3,2},{4,3},{5,4},{6,5},{7,6},{8,7},{9,8},{10,9},{11,1... | collective-permute-start | bytes 506888 | tf_op jit(solution)/shard_map/ppermute | solution.py:17
  23.9 10.0 %copy-start = (bf16[33,2,8,256]{3,2,1,0:T(8,128)(2,1)S(1)}, bf16[33,2,8,256]{3,2,1,0:T(8,128)(2,1)}, u32[]{:S(2)}) copy-start(bf16[33,2,8,256]{3,2,1,0:T(8,128)(2,1)} %param.12) | copy-start | bytes 811012
  35.3 2.0 copy-start.9
  38.9 0.8 copy-start.7
  40.5 94.4 %copy-start.1 = (f32[256]{0:T(256)S(1)}, f32[256]{0:T(256)}, u32[]{:S(2)}) copy-start(f32[256]{0:T(256)} %param.17) | copy-start | bytes 3076
  40.5 94.4 %copy-start.2 = (f32[256]{0:T(256)S(1)}, f32[256]{0:T(256)}, u32[]{:S(2)}) copy-start(f32[256]{0:T(256)} %param.16) | copy-start | bytes 3076
  135.5 6.1 %collective-permute-start.4 = (bf16[6,1,128,256]{3,2,1,0:T(8,128)(2,1)S(1)}, bf16[6,1,128,256]{3,2,1,0:T(8,128)(2,1)S(1)}, u32[]{:S(2)}, u32[]{:S(2)}) collective-permute-start(bf16[6,1,128,256]{3,2,1,0:T(8,128)(2,1)S(1)} %get-tuple-element.35), channel_id=1, source_target_pairs={{0,1},{1,2},{2,3},{3,4},{4,5},{5,6},{6,7},{7,8},{8,9},{9,10},{10,1... | collective-permute-start | bytes 1179656 | tf_op jit(solution)/shard_map/ppermute | solution.py:16
  136.9 8.8 %collective-permute-start.5 = (bf16[6,1,128,256]{3,2,1,0:T(8,128)(2,1)S(1)}, bf16[6,1,128,256]{3,2,1,0:T(8,128)(2,1)S(1)}, u32[]{:S(2)}, u32[]{:S(2)}) collective-permute-start(bf16[6,1,128,256]{3,2,1,0:T(8,128)(2,1)S(1)} %get-tuple-element.36), channel_id=1, source_target_pairs={{1,0},{2,1},{3,2},{4,3},{5,4},{6,5},{7,6},{8,7},{9,8},{10,9},{11,1... | collective-permute-start | bytes 1179656 | tf_op jit(solution)/shard_map/ppermute | solution.py:17
  138.2 252.4 %all-gather.5.cloned.1.call-start = ((), (), s32[]{:S(2)}) async-start(), calls=%async_computation.2 | async-start | bytes 1216512 | tf_op jit(solution)/shard_map/all_gather | solution.py:59
  153.5 66.9 %copy-start.10 = (f32[256]{0:T(256)S(1)}, f32[256]{0:T(256)}, u32[]{:S(2)}) copy-start(f32[256]{0:T(256)} %param.19) | copy-start | bytes 3076
  227.3 66.1 %copy-start.3 = (f32[256]{0:T(256)S(1)}, f32[256]{0:T(256)}, u32[]{:S(2)}) copy-start(f32[256]{0:T(256)} %param.21) | copy-start | bytes 3076
  227.3 66.1 %copy-start.5 = (f32[256]{0:T(256)S(1)}, f32[256]{0:T(256)}, u32[]{:S(2)}) copy-start(f32[256]{0:T(256)} %param.20) | copy-start | bytes 3076
  294.9 6.4 %collective-permute-start.6 = (bf16[6,1,128,256]{3,2,1,0:T(8,128)(2,1)}, bf16[6,1,128,256]{3,2,1,0:T(8,128)(2,1)}, u32[]{:S(2)}, u32[]{:S(2)}) collective-permute-start(bf16[6,1,128,256]{3,2,1,0:T(8,128)(2,1)} %get-tuple-element.33), channel_id=1, source_target_pairs={{0,1},{1,2},{2,3},{3,4},{4,5},{5,6},{6,7},{7,8},{8,9},{9,10},{10,1... | collective-permute-start | bytes 1179656 | tf_op jit(solution)/shard_map/ppermute | solution.py:16
  297.0 9.1 %collective-permute-start.7 = (bf16[6,1,128,256]{3,2,1,0:T(8,128)(2,1)}, bf16[6,1,128,256]{3,2,1,0:T(8,128)(2,1)S(1)}, u32[]{:S(2)}, u32[]{:S(2)}) collective-permute-start(bf16[6,1,128,256]{3,2,1,0:T(8,128)(2,1)} %get-tuple-element.34), channel_id=1, source_target_pairs={{1,0},{2,1},{3,2},{4,3},{5,4},{6,5},{7,6},{8,7},{9,8},{10,9},{11,1... | collective-permute-start | bytes 1179656 | tf_op jit(solution)/shard_map/ppermute | solution.py:17
  309.1 4.2 %copy-start.4 = (f32[256]{0:T(256)S(1)}, f32[256]{0:T(256)}, u32[]{:S(2)}) copy-start(f32[256]{0:T(256)} %param.21) | copy-start | bytes 3076
  309.1 4.2 %copy-start.6 = (f32[256]{0:T(256)S(1)}, f32[256]{0:T(256)}, u32[]{:S(2)}) copy-start(f32[256]{0:T(256)} %param.20) | copy-start | bytes 3076
  316.0 74.7 %copy-start.11 = (f32[256]{0:T(256)S(1)}, f32[256]{0:T(256)}, u32[]{:S(2)}) copy-start(f32[256]{0:T(256)} %param.23) | copy-start | bytes 3076
  390.6 5.4 %copy-start.8 = (pred[6]{0:T(512)(128)(4,1)S(1)}, pred[6]{0:T(512)(128)(4,1)}, u32[]{:S(2)}) copy-start(pred[6]{0:T(512)(128)(4,1)} %iota_compare_fusion.4) | copy-start | bytes 22
Sparse Core Ops, SparseCore 0:
  138.3 82.0 all-gather.2
  298.7 91.8 all-gather.4
where the time goes:
time: 408 us; the launch traced here: 404 us
  waiting for transfers between devices  158 us (39%)
  blocking collectives  152 us (37%)
  other arithmetic  24.1 us (6%)
  local copies, waits for them, and re-layouts  24.1 us (6%)
  starting transfers between devices  19.1 us (5%)
  between operations  13.9 us (3%)
  matrix products  13.1 us (3%)
    all_gather x2, waiting for transfers between devices, convolve(): lax.all_gather(weight_shard, 'height', axis=0, tiled=True)  135 us
    psum x2, blocking collectives, totals(): return lax.psum((part_sum, part_sq), 'height')  120 us
    all_to_all x1, blocking collectives, per_device(): lax.all_to_all(retained, 'frame', split_axis=0, concat_axis=2, tiled=True)  32.5 us
    unnamed x47, local copies, waits for them, and re-layouts  13.3 us
    ppermute x4, waiting for transfers between devices, with_halo(): after = lax.ppermute(first, axis, down)  13.1 us
    dot_general x2, matrix products, convolve(): jnp.dot(patches, lax.all_gather(weight_shard, 'height', axis=0, tiled=Tru...  10.7 us
    ppermute x4, starting transfers between devices, with_halo(): before = lax.ppermute(last, axis, up)  10.1 us
    ppermute x4, waiting for transfers between devices, with_halo(): before = lax.ppermute(last, axis, up)  9.2 us
  transfers between devices with their start and end apart: 10, of which 8 were waited for; matrix products, arithmetic and copies ran while one was open for 7% of the time, Pallas kernels for 0%

commit v1 on v0

v1 whole, which is shorter than its diff:
```python
import functools

import jax
import jax.numpy as jnp
from jax import lax
from jax.experimental import pallas as pl
from jax.experimental.pallas import tpu as pltpu
from jax.sharding import PartitionSpec as P

GROUPS = 32
C = 256
J = 8
MOST = 6
F32 = jnp.float32
BF16 = jnp.bfloat16
HIGH = lax.Precision.HIGHEST
MESH = pl.DeviceIdType.MESH
SUM_LANES = 128


def silu(v):
    half = 0.5 * v
    return half * jnp.tanh(half) + half


def hdot(a, b):
    return jnp.dot(a, b, precision=HIGH, preferred_element_type=F32)


def one_hot(rows, cols, fn):
    r = lax.broadcasted_iota(jnp.int32, (rows, cols), 0)
    c = lax.broadcasted_iota(jnp.int32, (rows, cols), 1)
    return jnp.where(fn(r, c), 1.0, 0.0).astype(F32)


def kernel(
    nf, nx, ny, frames, su, cells,
    counts, video, tw, w1, w2, tb, g1, s1, b1, g2, s2, b2,
    out,
    vid, twv, rowb, colb, hr, hc, gt, se, tc, bs, stage, sts, rs, ysc, xsc, fsb,
    rec, ha, hb, first, g4, so, wb, wr, stat, mu, sc, outv, offs,
    local_sem, p1_send, p1_recv, wl_sem, wy_send, wy_recv, wx_send, wx_recv, wp_send, wp_recv,
    a2a_send, a2a_recv, st_send, st_recv, y_send, y_recv, x_send, x_recv,
    ha_send, ha_recv, hb_send, hb_recv, out_sem,
):
    nh = nx * ny
    tp = frames + 1
    wide = tp * J
    fr = bs.shape[0]
    width = nf * J
    f = lax.axis_index("frame")
    h = lax.axis_index("height")
    x = h // ny
    y = lax.rem(h, ny)
    core = lax.rem(f, 2)
    hup, hdn = lax.rem(h + nh - 1, nh), lax.rem(h + 1, nh)
    fl, fr_ = lax.rem(f + nf - 1, nf), lax.rem(f + 1, nf)

    def dev(hh, ff):
        return {"height": hh, "frame": ff}

    def remote(src, dst, send, recv, hh, ff):
        return pltpu.make_async_remote_copy(
            src_ref=src, dst_ref=dst, send_sem=send, recv_sem=recv,
            device_id=dev(hh, ff), device_id_type=MESH,
        )

    def await_bytes(ref, sem):
        pltpu.make_async_copy(ref, ref, sem).wait()

    barrier = pltpu.get_barrier_semaphore()

    def greet(hh, ff):
        pl.semaphore_signal(barrier, inc=1, device_id=dev(hh, ff), device_id_type=MESH)

    for hh, ff in ((hup, f), (hdn, f), (hup, fl), (hup, fr_), (hdn, fl), (hdn, fr_)):
        greet(hh, ff)
    for s in range(1, ny):
        greet(x * ny + lax.rem(y + s, ny), f)
    for s in range(1, nx):
        greet(lax.rem(x + s, nx) * ny + y, f)
    for s in range(1, nf):
        greet(h, lax.rem(f + s, nf))
    greeted = 6 + (ny - 1) + (nx - 1) + (nf - 1)

    copy_video = pltpu.make_async_copy(video, vid, local_sem.at[0])
    copy_video.start()
    copy_tw = pltpu.make_async_copy(tw, twv, local_sem.at[1])
    copy_tw.start()
    lane0 = pl.multiple_of(core * 128, 128)
    lanes = pl.ds(lane0, 128)
    mine = pl.ds(h * su, su)
    own_w = [
        pltpu.make_async_copy(w.at[:, :, lanes], wb.at[i, mine, :, lanes], wl_sem.at[i])
        for i, w in enumerate((w1, w2))
    ]
    for copy in own_w:
        copy.start()

    total = jnp.int32(0)
    for k in range(nf):
        offs[k] = total
        total = total + counts[k]

    zero8 = jnp.zeros((8, C), F32)
    gt[0:8, :] = zero8
    gt[8 + wide : 16 + wide, :] = zero8
    g4[0:8, :] = zero8
    g4[8 + width : 16 + width, :] = zero8
    for a in range(3):
        for i in range(2):
            tc[a, i, 0:16, :] = jnp.zeros((16, C), F32)

    pick_left = one_hot(fr, wide, lambda r, c: c == r * J).astype(BF16)
    pick_right = one_hot(fr, wide, lambda r, c: c == r * J + J - 1).astype(BF16)

    copy_video.wait()
    for i in range(2):
        act = silu(vid[:, i].astype(F32)).astype(BF16)
        rowb[i, 0:frames] = act
        rowb[i, frames:tp] = jnp.zeros((1, J, C), BF16)
        flat = rowb[i].astype(F32).reshape(wide, C).astype(BF16)
        colb[0, i] = jnp.dot(pick_left, flat, preferred_element_type=F32).astype(BF16)
        colb[1, i] = jnp.dot(pick_right, flat, preferred_element_type=F32).astype(BF16)

    pl.semaphore_wait(barrier, greeted)

    borders = [
        (rowb.at[0], hr.at[1], hup, f),
        (rowb.at[1], hr.at[0], hdn, f),
        (colb.at[0], hc.at[1, 1:3], h, fl),
        (colb.at[1], hc.at[0, 1:3], h, fr_),
        (colb.at[0, 0], hc.at[1, 3], hup, fl),
        (colb.at[1, 0], hc.at[0, 3], hup, fr_),
        (colb.at[0, 1], hc.at[1, 0], hdn, fl),
        (colb.at[1, 1], hc.at[0, 0], hdn, fr_),
    ]
    p1 = [
        remote(src, dst, p1_send.at[n], p1_recv.at[n], hh, ff)
        for n, (src, dst, hh, ff) in enumerate(borders)
    ]
    for copy in p1:
        copy.start()

    for copy in own_w:
        copy.wait()
    for i in range(2):
        for s in range(1, ny):
            here = wb.at[i, mine, :, lanes]
            remote(
                here, here, wy_send.at[i], wy_recv.at[i], x * ny + lax.rem(y + s, ny), f
            ).start()

    for copy in p1:
        copy.wait()

    put_left = one_hot(wide, fr, lambda r, c: r == c * J).astype(BF16)
    put_right = one_hot(wide, fr, lambda r, c: r == c * J + J - 1).astype(BF16)
    col = lax.rem(lax.broadcasted_iota(jnp.int32, (wide, C), 0), J)
    keep_left = jnp.where(f > 0, 1.0, 0.0)
    keep_right = jnp.where(f < nf - 1, 1.0, 0.0)
    keep_top = jnp.where(h > 0, 1.0, 0.0)
    keep_bottom = jnp.where(h < nh - 1, 1.0, 0.0)
    for ip in range(4):
        source = (hr.at[0], rowb.at[0], rowb.at[1], hr.at[1])[ip]
        keep = (keep_top, 1.0, 1.0, keep_bottom)[ip]
        middle = source[...].astype(F32).reshape(wide, C) * keep
        gt[8 : 8 + wide, :] = middle
        lefts = jnp.dot(put_left, hc[0, ip], preferred_element_type=F32) * (keep * keep_left)
        rights = jnp.dot(put_right, hc[1, ip], preferred_element_type=F32) * (keep * keep_right)
        rows = slice(ip * wide, (ip + 1) * wide)
        se[rows, 0:C] = jnp.where(col == 0, lefts, gt[7 : 7 + wide, :]).astype(BF16)
        se[rows, C : 2 * C] = middle.astype(BF16)
        se[rows, 2 * C : 3 * C] = jnp.where(col == J - 1, rights, gt[9 : 9 + wide, :]).astype(BF16)
    copy_tw.wait()

    def taps(a, carry):
        for i in range(2):
            acc = jnp.zeros((wide, C), F32)
            for b in range(3):
                start = pl.multiple_of(a * (9 * C) + b * (3 * C), 3 * C)
                acc = acc + jnp.dot(
                    se[(i + b) * wide : (i + b + 1) * wide, :],
                    twv[pl.ds(start, 3 * C), :],
                    preferred_element_type=F32,
                )
            tc[a, i, 16 : 16 + wide, :] = acc
        return carry

    lax.fori_loop(0, 3, taps, 0)

    n_all = frames * J
    sums = jnp.zeros((n_all, C), F32)
    squares = jnp.zeros((n_all, C), F32)
    for i in range(2):
        value = (
            vid[:, i].astype(F32).reshape(n_all, C)
            + (tc[0, i, 0:n_all, :] + tc[1, i, 8 : 8 + n_all, :] + tc[2, i, 16 : 16 + n_all, :])
            + tb[...]
        )
        bs[0:frames, i] = value.reshape(frames, J, C).astype(BF16)
        rounded = bs[0:frames, i].astype(F32).reshape(n_all, C)
        sums = sums + rounded
        squares = squares + rounded * rounded
        bs[frames:fr, i] = jnp.zeros((fr - frames, J, C), BF16)

    per = C // GROUPS
    sum_map = one_hot(C, SUM_LANES, lambda r, c: c == r // per)
    sq_map = one_hot(C, SUM_LANES, lambda r, c: c == r // per + GROUPS)
    fsum = jnp.sum(sums.reshape(frames, J, C), axis=1)
    fsq = jnp.sum(squares.reshape(frames, J, C), axis=1)
    fsb[0:frames, :] = hdot(fsum, sum_map) + hdot(fsq, sq_map)
    fsb[frames:fr, :] = jnp.zeros((fr - frames, SUM_LANES), F32)

    def pack(k, carry):
        start = offs[k]
        sts[k] = fsb[pl.ds(start, 8), :]
        for r in range(MOST):
            stage[r, k] = bs[start + r]
        return carry

    lax.fori_loop(0, nf, pack, 0)

    def send_sums(s, carry):
        k = lax.rem(f + s, nf)
        remote(sts.at[k], rs.at[f], st_send, st_recv, h, k).start()
        return carry

    lax.fori_loop(1, nf, send_sums, 0)

    def send_slot(n, carry):
        r = n // (nf - 1)
        k = lax.rem(f + 1 + lax.rem(n, nf - 1), nf)
        remote(stage.at[r, k], rec.at[r, :, f], a2a_send, a2a_recv.at[r], h, k).start()
        return carry

    lax.fori_loop(0, MOST * (nf - 1), send_slot, 0)
    my_offset = offs[f]
    rs[f] = fsb[pl.ds(my_offset, 8), :]
    for r in range(MOST):
        rec[r, :, f] = bs[my_offset + r]

    block = pl.ds(x * (ny * su), ny * su)
    for i in range(2):
        await_bytes(wb.at[i, pl.ds(0, (ny - 1) * su), :, lanes], wy_recv.at[i])
        for s in range(1, nx):
            here = wb.at[i, block, :, lanes]
            remote(
                here, here, wx_send.at[i], wx_recv.at[i], lax.rem(x + s, nx) * ny + y, f
            ).start()

    def y_start(q, value):
        ysc[q, y] = value
        for s in range(1, ny):
            remote(
                ysc.at[q, y], ysc.at[q, y], y_send.at[q], y_recv.at[q],
                x * ny + lax.rem(y + s, ny), f,
            ).start()

    def y_finish(q):
        await_bytes(ysc.at[q, 0 : ny - 1], y_recv.at[q])
        return jnp.sum(ysc[q], axis=0)

    def x_start(q, value):
        xsc[q, x] = value
        for s in range(1, nx):
            remote(
                xsc.at[q, x], xsc.at[q, x], x_send.at[q], x_recv.at[q],
                lax.rem(x + s, nx) * ny + y, f,
            ).start()

    def x_finish(q):
        await_bytes(xsc.at[q, 0 : nx - 1], x_recv.at[q])
        return jnp.sum(xsc[q], axis=0)

    def set_norm(q, totals, gain):
        sum_back = one_hot(SUM_LANES, C, lambda r, c: r == c // per)
        sq_back = one_hot(SUM_LANES, C, lambda r, c: r == c // per + GROUPS)
        mean = hdot(totals, sum_back) / cells
        var = hdot(totals, sq_back) / cells - mean * mean
        mu[q] = mean
        sc[q] = lax.rsqrt(jnp.maximum(var, 0.0) + 1e-06) * gain

    await_bytes(rs.at[0 : nf - 1], st_recv)
    y_start(0, jnp.sum(rs[...], axis=0))
    x_start(0, y_finish(0))
    set_norm(0, x_finish(0), g1[...])

    partner = f + 1 - 2 * core
    for i in range(2):
        await_bytes(wb.at[i, pl.ds(0, (nx - 1) * ny * su), :, lanes], wx_recv.at[i])
        half = wb.at[i, :, :, lanes]
        remote(half, half, wp_send.at[i], wp_recv.at[i], h, partner).start()

    other = pl.ds(pl.multiple_of(128 - core * 128, 128), 128)

    def ready_weight(i):
        await_bytes(wb.at[i, :, :, other], wp_recv.at[i])
        step = 18

        def widen(n, carry):
            rows = wb[i, pl.ds(n * step, step)].astype(F32).reshape(step * 8, C)
            wr[i, pl.ds(pl.multiple_of(n * step * 8, step * 8), step * 8), :] = rows.astype(BF16)
            return carry

        lax.fori_loop(0, nh * su // step, widen, 0)

    def slot_in(r):
        await_bytes(rec.at[r, :, 0 : nf - 1], a2a_recv.at[r])
        remote(rec.at[r, 0], ha.at[r, 1], ha_send.at[r, 0], ha_recv.at[r, 0], hup, f).start()
        remote(rec.at[r, 1], ha.at[r, 0], ha_send.at[r, 1], ha_recv.at[r, 1], hdn, f).start()

    keeps = (keep_top, None, None, keep_bottom)

    def convolve(r, rows_of, q, shift, weight):
        mean = mu[q, pl.ds(r, 1), :]
        scale = sc[q, pl.ds(r, 1), :]
        for ip in range(4):
            normed = silu((rows_of(ip) - mean) * scale + shift)
            if keeps[ip] is not None:
                normed = normed * keeps[ip]
            g4[8 : 8 + width, :] = normed
            rows = slice(ip * width, (ip + 1) * width)
            so[rows, 0:C] = g4[7 : 7 + width, :].astype(BF16)
            so[rows, C : 2 * C] = normed.astype(BF16)
            so[rows, 2 * C : 3 * C] = g4[9 : 9 + width, :].astype(BF16)
        acc = jnp.zeros((2 * width, C), F32)
        for b in range(3):
            acc = acc + jnp.dot(
                so[b * width : (b + 2) * width, :],
                wr[weight, b * 3 * C : (b + 1) * 3 * C, :],
                preferred_element_type=F32,
            )
        return acc

    def first_rows(r):
        def get(ip):
            ref = (ha.at[r, 0], rec.at[r, 0], rec.at[r, 1], ha.at[r, 1])[ip]
            return ref[...].astype(F32).reshape(width, C)

        return get

    def second_rows(r):
        def get(ip):
            ref = (hb.at[r, 0], first.at[r, 0], first.at[r, 1], hb.at[r, 1])[ip]
            return ref[...].astype(F32)

        return get

    stat[...] = jnp.zeros_like(stat)
    ready_weight(0)
    slot_in(0)

    def first_conv(r, carry):
        @pl.when(r + 1 < MOST)
        def _():
            slot_in(r + 1)

        await_bytes(ha.at[r, 0], ha_recv.at[r, 0])
        await_bytes(ha.at[r, 1], ha_recv.at[r, 1])
        result = convolve(r, first_rows(r), 0, s1[...], 0) + b1[...]
        first[r, 0] = result[0:width].astype(BF16)
        first[r, 1] = result[width : 2 * width].astype(BF16)
        remote(first.at[r, 0], hb.at[r, 1], hb_send.at[r, 0], hb_recv.at[r, 0], hup, f).start()
        remote(first.at[r, 1], hb.at[r, 0], hb_send.at[r, 1], hb_recv.at[r, 1], hdn, f).start()
        rounded = first[r, 0].astype(F32), first[r, 1].astype(F32)
        sums = rounded[0] + rounded[1]
        squares = rounded[0] * rounded[0] + rounded[1] * rounded[1]
        stat[0, pl.ds(r, 1), :] = jnp.sum(sums, axis=0, keepdims=True)
        stat[1, pl.ds(r, 1), :] = jnp.sum(squares, axis=0, keepdims=True)
        return carry

    lax.fori_loop(0, MOST, first_conv, 0)
    y_start(1, hdot(stat[0], sum_map) + hdot(stat[1], sq_map))
    ready_weight(1)
    x_start(1, y_finish(1))
    set_norm(1, x_finish(1), g2[...])

    my_count = counts[f]

    def second_conv(r, carry):
        await_bytes(hb.at[r, 0], hb_recv.at[r, 0])
        await_bytes(hb.at[r, 1], hb_recv.at[r, 1])
        result = convolve(r, second_rows(r), 1, s2[...], 1) + b2[...]
        live = r < my_count
        for i in range(2):
            kept = rec[r, i].astype(F32).reshape(width, C)
            value = kept + result[i * width : (i + 1) * width]
            outv[r, i] = jnp.where(live, value, 0.0).astype(BF16)
        pltpu.make_async_copy(outv.at[r], out.at[r], out_sem.at[r]).start()
        return carry

    lax.fori_loop(0, MOST, second_conv, 0)

    for i in range(2):
        await_bytes(wb.at[i, pl.ds(0, (ny - 1) * su), :, lanes], wy_send.at[i])
        await_bytes(wb.at[i, pl.ds(0, (nx - 1) * ny * su), :, lanes], wx_send.at[i])
        await_bytes(wb.at[i, :, :, lanes], wp_send.at[i])
    await_bytes(sts.at[0 : nf - 1], st_send)
    await_bytes(stage.at[:, 0 : nf - 1], a2a_send)
    for q in range(2):
        await_bytes(ysc.at[q, 0 : ny - 1], y_send.at[q])
        await_bytes(xsc.at[q, 0 : nx - 1], x_send.at[q])
    for r in range(MOST):
        for i in range(2):
            await_bytes(rec.at[r, i], ha_send.at[r, i])
            await_bytes(first.at[r, i], hb_send.at[r, i])
        pltpu.make_async_copy(outv.at[r], out.at[r], out_sem.at[r]).wait()


def per_device(nf, nh, video, counts, tw, tb, g1, s1, w1, b1, g2, s2, w2, b2):
    frames = video.shape[0]
    ny = 8 if nh % 8 == 0 else 2
    nx = nh // ny
    su = w1.shape[0] // 8
    tp = frames + 1
    wide = tp * J
    fr = -(-(frames + 7) // 8) * 8
    width = nf * J
    cells = float(2 * nh * width * (C // GROUPS))
    row = lambda v: v.reshape(1, C)
    vm = pl.BlockSpec(memory_space=pltpu.VMEM)
    anyspace = pl.BlockSpec(memory_space=pl.ANY)
    dma = pltpu.SemaphoreType.DMA
    V = pltpu.VMEM
    scratch = [
        V((frames, 2, J, C), BF16),
        V((27 * C, C), BF16),
        V((2, tp, J, C), BF16),
        V((2, 2, fr, C), BF16),
        V((2, tp, J, C), BF16),
        V((2, 4, fr, C), BF16),
        V((wide + 16, C), F32),
        V((4 * wide, 3 * C), BF16),
        V((3, 2, wide + 16, C), F32),
        V((fr, 2, J, C), BF16),
        V((MOST, nf, 2, J, C), BF16),
        V((nf, 8, SUM_LANES), F32),
        V((nf, 8, SUM_LANES), F32),
        V((2, ny, 8, SUM_LANES), F32),
        V((2, nx, 8, SUM_LANES), F32),
        V((fr, SUM_LANES), F32),
        V((MOST, 2, nf, J, C), BF16),
        V((MOST, 2, nf, J, C), BF16),
        V((MOST, 2, width, C), BF16),
        V((MOST, 2, width, C), BF16),
        V((width + 16, C), F32),
        V((4 * width, 3 * C), BF16),
        V((2, nh * su, 8, C), BF16),
        V((2, 9 * C, C), BF16),
        V((2, 8, C), F32),
        V((2, 8, C), F32),
        V((2, 8, C), F32),
        V((MOST, 2, width, C), BF16),
        pltpu.SMEM((nf,), jnp.int32),
        dma((2,)), dma((8,)), dma((8,)), dma((2,)),
        dma((2,)), dma((2,)), dma((2,)), dma((2,)), dma((2,)), dma((2,)),
        dma, dma((MOST,)), dma, dma, dma((2,)), dma((2,)), dma((2,)), dma((2,)),
        dma((MOST, 2)), dma((MOST, 2)), dma((MOST, 2)), dma((MOST, 2)), dma((MOST,)),
    ]
    return pl.pallas_call(
        functools.partial(kernel, nf, nx, ny, frames, su, cells),
        out_shape=jax.ShapeDtypeStruct((MOST, 2, width, C), BF16),
        in_specs=[pl.BlockSpec(memory_space=pltpu.SMEM)] + [anyspace] * 4 + [vm] * 7,
        out_specs=anyspace,
        scratch_shapes=scratch,
        compiler_params=pltpu.CompilerParams(
            collective_id=0, has_side_effects=True, vmem_limit_bytes=60 * 2**20
        ),
        name="block",
    )(
        counts, video, tw, w1.reshape(su, 8, C), w2.reshape(su, 8, C),
        row(tb), row(g1), row(s1), row(b1), row(g2), row(s2), row(b2),
    )


def solution(mesh):
    placed = (
        P(None, "height", "frame", None),
        P(), P(), P(), P(), P(),
        P("height", None),
        P(), P(), P(),
        P("height", None),
        P(),
    )
    return jax.shard_map(
        functools.partial(per_device, mesh.shape["frame"], mesh.shape["height"]),
        mesh=mesh,
        in_specs=placed,
        out_specs=P("frame", "height", None, None),
        check_vma=False,
    )
```

time: 408 us -> 82.6 us (0.20)
  the two profiles are of different devices: /device:TPU:1 before, /device:TPU:8 now
where the time goes in v1:
time: 82.6 us; the launch traced here: 82.5 us
  Pallas kernels  80.4 us (97%)
  local copies, waits for them, and re-layouts  2.06 us (2%)
    pallas_call x1, Pallas kernels, per_device(): pl.pallas_call(functools.partial(kernel, nf, nx, ny, frames, su, cells),...  80.4 us
    unnamed x1, local copies, waits for them, and re-layouts  2.06 us

profile of v1, /device:TPU:8, one launch (start us, length us, event | category | flops | bytes accessed | tf_op | source)
XLA Modules:
  0.0 82.5 jit_solution(9828454795087308438)
XLA Ops:
  0.0 80.4 %block.1 = bf16[6,2,128,256]{3,2,1,0:T(8,128)(2,1)} custom-call(s32[16]{0:T(128)} %counts.1, bf16[33,2,8,256]{3,2,1,0:T(8,128)(2,1)} %video.1, bf16[6912,256]{1,0:T(8,128)(2,1)} %tw.1, bf16[9,8,256]{2,1,0:T(8,128)(2,1)} %bitcast.9, bf16[9,8,256]{2,1,0:T(8,128)(2,1)} %bitcast.10, f32[1,256]{1,0:T(1,128)} %bitcast.11, f32[1,256]{1,0:T(1,128)} %bitcast.12, ...), custom_call_target="tpu_custom_call" | custom-call | tf_op jit(solution)/shard_map/block/pallas_call | solution.py:461
  80.4 2.1 %copy.14 = bf16[6,2,128,256]{3,2,1,0:T(8,128)(2,1)} copy(bf16[6,2,128,256]{3,2,1,0:T(8,128)(2,1)} %block.1) | data formatting | bytes 1572864

commit v2 on v1

--- a/solution.py
+++ b/solution.py
@@ -35,13 +35,13 @@
 
 def kernel(
     nf, nx, ny, frames, su, cells,
-    counts, video, tw, w1, w2, tb, g1, s1, b1, g2, s2, b2,
+    counts, video, tw, w1, w2, tb_in, g1_in, s1_in, b1_in, g2_in, s2_in, b2_in,
     out,
     vid, twv, rowb, colb, hr, hc, gt, se, tc, bs, stage, sts, rs, ysc, xsc, fsb,
-    rec, ha, hb, first, g4, so, wb, wr, stat, mu, sc, outv, offs,
+    rec, ha, hb, first, g4, so, wb, wr, stat, mu, sc, outv, pv, offs,
     local_sem, p1_send, p1_recv, wl_sem, wy_send, wy_recv, wx_send, wx_recv, wp_send, wp_recv,
     a2a_send, a2a_recv, st_send, st_recv, y_send, y_recv, x_send, x_recv,
-    ha_send, ha_recv, hb_send, hb_recv, out_sem,
+    ha_send, ha_recv, hb_send, hb_recv, out_sem, pv_sem, known,
 ):
     nh = nx * ny
     tp = frames + 1
@@ -70,18 +70,23 @@
 
     barrier = pltpu.get_barrier_semaphore()
 
-    def greet(hh, ff):
-        pl.semaphore_signal(barrier, inc=1, device_id=dev(hh, ff), device_id_type=MESH)
-
-    for hh, ff in ((hup, f), (hdn, f), (hup, fl), (hup, fr_), (hdn, fl), (hdn, fr_)):
-        greet(hh, ff)
-    for s in range(1, ny):
-        greet(x * ny + lax.rem(y + s, ny), f)
-    for s in range(1, nx):
-        greet(lax.rem(x + s, nx) * ny + y, f)
-    for s in range(1, nf):
-        greet(h, lax.rem(f + s, nf))
-    greeted = 6 + (ny - 1) + (nx - 1) + (nf - 1)
+    def greet(sem, hh, ff):
+        pl.semaphore_signal(sem, inc=1, device_id=dev(hh, ff), device_id_type=MESH)
+
+    def on_z(s):
+        return h, lax.rem(f + nf + s, nf)
+
+    def on_y(s):
+        return x * ny + lax.rem(y + ny + s, ny), f
+
+    def on_x(s):
+        return lax.rem(x + nx + s, nx) * ny + y, f
+
+    near = [(hup, f), (hdn, f), (hup, fl), (hup, fr_), (hdn, fl), (hdn, fr_)]
+    for step in (-1, 1):
+        near += [on_z(step), on_y(step), on_x(step)]
+    for hh, ff in near:
+        greet(barrier, hh, ff)
 
     copy_video = pltpu.make_async_copy(video, vid, local_sem.at[0])
     copy_video.start()
@@ -97,6 +102,14 @@
     for copy in own_w:
         copy.start()
 
+    vectors = [
+        pltpu.make_async_copy(v, pv.at[n], pv_sem.at[n])
+        for n, v in enumerate((tb_in, g1_in, s1_in, b1_in, g2_in, s2_in, b2_in))
+    ]
+    for copy in vectors:
+        copy.start()
+    tb, g1, s1, b1, g2, s2, b2 = (pv.at[n] for n in range(7))
+
     total = jnp.int32(0)
     for k in range(nf):
         offs[k] = total
@@ -123,7 +136,7 @@
         colb[0, i] = jnp.dot(pick_left, flat, preferred_element_type=F32).astype(BF16)
         colb[1, i] = jnp.dot(pick_right, flat, preferred_element_type=F32).astype(BF16)
 
-    pl.semaphore_wait(barrier, greeted)
+    pl.semaphore_wait(barrier, len(near))
 
     borders = [
         (rowb.at[0], hr.at[1], hup, f),
@@ -142,17 +155,27 @@
     for copy in p1:
         copy.start()
 
+    rings = ((on_z, nf), (on_y, ny), (on_x, nx))
+    reach = 1
+    while reach < nf // 2:
+        for n, (on, size) in enumerate(rings):
+            if reach < size // 2:
+                for step in (-reach, reach):
+                    greet(known.at[n, reach // 2], *on(step))
+        for n, (on, size) in enumerate(rings):
+            if reach < size // 2:
+                pl.semaphore_wait(known.at[n, reach // 2], 2)
+        reach *= 2
+
+    for copy in p1:
+        copy.wait()
+
     for copy in own_w:
         copy.wait()
     for i in range(2):
         for s in range(1, ny):
             here = wb.at[i, mine, :, lanes]
-            remote(
-                here, here, wy_send.at[i], wy_recv.at[i], x * ny + lax.rem(y + s, ny), f
-            ).start()
-
-    for copy in p1:
-        copy.wait()
+            remote(here, here, wy_send.at[i], wy_recv.at[i], *on_y(s)).start()
 
     put_left = one_hot(wide, fr, lambda r, c: r == c * J).astype(BF16)
     put_right = one_hot(wide, fr, lambda r, c: r == c * J + J - 1).astype(BF16)
@@ -173,6 +196,8 @@
         se[rows, C : 2 * C] = middle.astype(BF16)
         se[rows, 2 * C : 3 * C] = jnp.where(col == J - 1, rights, gt[9 : 9 + wide, :]).astype(BF16)
     copy_tw.wait()
+    for copy in vectors:
+        copy.wait()
 
     def taps(a, carry):
         for i in range(2):
@@ -241,20 +266,27 @@
         rec[r, :, f] = bs[my_offset + r]
 
     block = pl.ds(x * (ny * su), ny * su)
-    for i in range(2):
+
+    def along_x(i):
         await_bytes(wb.at[i, pl.ds(0, (ny - 1) * su), :, lanes], wy_recv.at[i])
         for s in range(1, nx):
             here = wb.at[i, block, :, lanes]
-            remote(
-                here, here, wx_send.at[i], wx_recv.at[i], lax.rem(x + s, nx) * ny + y, f
-            ).start()
+            remote(here, here, wx_send.at[i], wx_recv.at[i], *on_x(s)).start()
+
+    partner = f + 1 - 2 * core
+    other = pl.ds(pl.multiple_of(128 - core * 128, 128), 128)
+
+    def to_partner(i):
+        await_bytes(wb.at[i, pl.ds(0, (nx - 1) * ny * su), :, lanes], wx_recv.at[i])
+        half = wb.at[i, :, :, lanes]
+        remote(half, half, wp_send.at[i], wp_recv.at[i], h, partner).start()
 
     def y_start(q, value):
         ysc[q, y] = value
         for s in range(1, ny):
             remote(
                 ysc.at[q, y], ysc.at[q, y], y_send.at[q], y_recv.at[q],
-                x * ny + lax.rem(y + s, ny), f,
+                *on_y(s),
             ).start()
 
     def y_finish(q):
@@ -266,7 +298,7 @@
         for s in range(1, nx):
             remote(
                 xsc.at[q, x], xsc.at[q, x], x_send.at[q], x_recv.at[q],
-                lax.rem(x + s, nx) * ny + y, f,
+                *on_x(s),
             ).start()
 
     def x_finish(q):
@@ -281,19 +313,6 @@
         mu[q] = mean
         sc[q] = lax.rsqrt(jnp.maximum(var, 0.0) + 1e-06) * gain
 
-    await_bytes(rs.at[0 : nf - 1], st_recv)
-    y_start(0, jnp.sum(rs[...], axis=0))
-    x_start(0, y_finish(0))
-    set_norm(0, x_finish(0), g1[...])
-
-    partner = f + 1 - 2 * core
-    for i in range(2):
-        await_bytes(wb.at[i, pl.ds(0, (nx - 1) * ny * su), :, lanes], wx_recv.at[i])
-        half = wb.at[i, :, :, lanes]
-        remote(half, half, wp_send.at[i], wp_recv.at[i], h, partner).start()
-
-    other = pl.ds(pl.multiple_of(128 - core * 128, 128), 128)
-
     def ready_weight(i):
         await_bytes(wb.at[i, :, :, other], wp_recv.at[i])
         step = 18
@@ -309,6 +328,16 @@
         await_bytes(rec.at[r, :, 0 : nf - 1], a2a_recv.at[r])
         remote(rec.at[r, 0], ha.at[r, 1], ha_send.at[r, 0], ha_recv.at[r, 0], hup, f).start()
         remote(rec.at[r, 1], ha.at[r, 0], ha_send.at[r, 1], ha_recv.at[r, 1], hdn, f).start()
+
+    along_x(0)
+    await_bytes(rs.at[0 : nf - 1], st_recv)
+    y_start(0, jnp.sum(rs[...], axis=0))
+    slot_in(0)
+    x_start(0, y_finish(0))
+    along_x(1)
+    slot_in(1)
+    set_norm(0, x_finish(0), g1[...])
+    to_partner(0)
 
     keeps = (keep_top, None, None, keep_bottom)
 
@@ -348,40 +377,60 @@
         return get
 
     stat[...] = jnp.zeros_like(stat)
-    ready_weight(0)
-    slot_in(0)
+    split = MOST - 2
+
+    def sums_start(q):
+        y_start(q, hdot(stat[0], sum_map) + hdot(stat[1], sq_map))
 
     def first_conv(r, carry):
-        @pl.when(r + 1 < MOST)
+        @pl.when(r + 2 < MOST)
         def _():
-            slot_in(r + 1)
+            slot_in(r + 2)
+
+        @pl.when(r == 0)
+        def _():
+            ready_weight(0)
 
         await_bytes(ha.at[r, 0], ha_recv.at[r, 0])
         await_bytes(ha.at[r, 1], ha_recv.at[r, 1])
         result = convolve(r, first_rows(r), 0, s1[...], 0) + b1[...]
         first[r, 0] = result[0:width].astype(BF16)
         first[r, 1] = result[width : 2 * width].astype(BF16)
-        remote(first.at[r, 0], hb.at[r, 1], hb_send.at[r, 0], hb_recv.at[r, 0], hup, f).start()
-        remote(first.at[r, 1], hb.at[r, 0], hb_send.at[r, 1], hb_recv.at[r, 1], hdn, f).start()
         rounded = first[r, 0].astype(F32), first[r, 1].astype(F32)
         sums = rounded[0] + rounded[1]
         squares = rounded[0] * rounded[0] + rounded[1] * rounded[1]
         stat[0, pl.ds(r, 1), :] = jnp.sum(sums, axis=0, keepdims=True)
         stat[1, pl.ds(r, 1), :] = jnp.sum(squares, axis=0, keepdims=True)
+
+        @pl.when(r == split - 1)
+        def _():
+            sums_start(1)
+
+        @pl.when(r == MOST - 1)
+        def _():
+            sums_start(2)
+
+        remote(first.at[r, 0], hb.at[r, 1], hb_send.at[r, 0], hb_recv.at[r, 0], hup, f).start()
+        remote(first.at[r, 1], hb.at[r, 0], hb_send.at[r, 1], hb_recv.at[r, 1], hdn, f).start()
+
+        @pl.when(r == split - 1)
+        def _():
+            to_partner(1)
+
         return carry
 
     lax.fori_loop(0, MOST, first_conv, 0)
-    y_start(1, hdot(stat[0], sum_map) + hdot(stat[1], sq_map))
+    x_start(1, y_finish(1))
     ready_weight(1)
-    x_start(1, y_finish(1))
+    x_start(2, y_finish(2))
     set_norm(1, x_finish(1), g2[...])
 
     my_count = counts[f]
 
-    def second_conv(r, carry):
+    def second_conv(q, r, carry):
         await_bytes(hb.at[r, 0], hb_recv.at[r, 0])
         await_bytes(hb.at[r, 1], hb_recv.at[r, 1])
-        result = convolve(r, second_rows(r), 1, s2[...], 1) + b2[...]
+        result = convolve(r, second_rows(r), q, s2[...], 1) + b2[...]
         live = r < my_count
         for i in range(2):
             kept = rec[r, i].astype(F32).reshape(width, C)
@@ -390,7 +439,9 @@
         pltpu.make_async_copy(outv.at[r], out.at[r], out_sem.at[r]).start()
         return carry
 
-    lax.fori_loop(0, MOST, second_conv, 0)
+    lax.fori_loop(0, split, functools.partial(second_conv, 1), 0)
+    set_norm(2, x_finish(2), g2[...])
+    lax.fori_loop(split, MOST, functools.partial(second_conv, 2), 0)
 
     for i in range(2):
         await_bytes(wb.at[i, pl.ds(0, (ny - 1) * su), :, lanes], wy_send.at[i])
@@ -398,7 +449,7 @@
         await_bytes(wb.at[i, :, :, lanes], wp_send.at[i])
     await_bytes(sts.at[0 : nf - 1], st_send)
     await_bytes(stage.at[:, 0 : nf - 1], a2a_send)
-    for q in range(2):
+    for q in range(3):
         await_bytes(ysc.at[q, 0 : ny - 1], y_send.at[q])
         await_bytes(xsc.at[q, 0 : nx - 1], x_send.at[q])
     for r in range(MOST):
@@ -419,7 +470,6 @@
     width = nf * J
     cells = float(2 * nh * width * (C // GROUPS))
     row = lambda v: v.reshape(1, C)
-    vm = pl.BlockSpec(memory_space=pltpu.VMEM)
     anyspace = pl.BlockSpec(memory_space=pl.ANY)
     dma = pltpu.SemaphoreType.DMA
     V = pltpu.VMEM
@@ -437,8 +487,8 @@
         V((MOST, nf, 2, J, C), BF16),
         V((nf, 8, SUM_LANES), F32),
         V((nf, 8, SUM_LANES), F32),
-        V((2, ny, 8, SUM_LANES), F32),
-        V((2, nx, 8, SUM_LANES), F32),
+        V((3, ny, 8, SUM_LANES), F32),
+        V((3, nx, 8, SUM_LANES), F32),
         V((fr, SUM_LANES), F32),
         V((MOST, 2, nf, J, C), BF16),
         V((MOST, 2, nf, J, C), BF16),
@@ -449,19 +499,21 @@
         V((2, nh * su, 8, C), BF16),
         V((2, 9 * C, C), BF16),
         V((2, 8, C), F32),
-        V((2, 8, C), F32),
-        V((2, 8, C), F32),
+        V((3, 8, C), F32),
+        V((3, 8, C), F32),
         V((MOST, 2, width, C), BF16),
+        V((7, 1, C), F32),
         pltpu.SMEM((nf,), jnp.int32),
         dma((2,)), dma((8,)), dma((8,)), dma((2,)),
         dma((2,)), dma((2,)), dma((2,)), dma((2,)), dma((2,)), dma((2,)),
-        dma, dma((MOST,)), dma, dma, dma((2,)), dma((2,)), dma((2,)), dma((2,)),
-        dma((MOST, 2)), dma((MOST, 2)), dma((MOST, 2)), dma((MOST, 2)), dma((MOST,)),
+        dma, dma((MOST,)), dma, dma, dma((3,)), dma((3,)), dma((3,)), dma((3,)),
+        dma((MOST, 2)), dma((MOST, 2)), dma((MOST, 2)), dma((MOST, 2)), dma((MOST,)), dma((7,)),
+        pltpu.SemaphoreType.REGULAR((3, 3)),
     ]
     return pl.pallas_call(
         functools.partial(kernel, nf, nx, ny, frames, su, cells),
         out_shape=jax.ShapeDtypeStruct((MOST, 2, width, C), BF16),
-        in_specs=[pl.BlockSpec(memory_space=pltpu.SMEM)] + [anyspace] * 4 + [vm] * 7,
+        in_specs=[pl.BlockSpec(memory_space=pltpu.SMEM)] + [anyspace] * 11,
         out_specs=anyspace,
         scratch_shapes=scratch,
         compiler_params=pltpu.CompilerParams(

time: 82.6 us -> 72.4 us (0.88)
  the two profiles are of different devices: /device:TPU:8 before, /device:TPU:1 now
where the time goes in v2:
time: 72.4 us; the launch traced here: 71.5 us
  Pallas kernels  69.5 us (96%)
  local copies, waits for them, and re-layouts  2.06 us (3%)
    pallas_call x1, Pallas kernels, per_device(): pl.pallas_call(functools.partial(kernel, nf, nx, ny, frames, su, cells),...  69.5 us
    unnamed x1, local copies, waits for them, and re-layouts  2.06 us

profile of v2, /device:TPU:1, one launch (start us, length us, event | category | flops | bytes accessed | tf_op | source)
XLA Modules:
  0.0 71.5 jit_solution(5716914402562184117)
XLA Ops:
  0.0 69.5 %block.1 = bf16[6,2,128,256]{3,2,1,0:T(8,128)(2,1)} custom-call(s32[16]{0:T(128)} %counts.1, bf16[33,2,8,256]{3,2,1,0:T(8,128)(2,1)} %video.1, bf16[6912,256]{1,0:T(8,128)(2,1)} %tw.1, bf16[9,8,256]{2,1,0:T(8,128)(2,1)} %bitcast.9, bf16[9,8,256]{2,1,0:T(8,128)(2,1)} %bitcast.10, f32[1,256]{1,0:T(1,128)} %bitcast.11, f32[1,256]{1,0:T(1,128)} %bitcast.12, ...), custom_call_target="tpu_custom_call" | custom-call | tf_op jit(solution)/shard_map/block/pallas_call | solution.py:513
  69.5 2.1 %copy.14 = bf16[6,2,128,256]{3,2,1,0:T(8,128)(2,1)} copy(bf16[6,2,128,256]{3,2,1,0:T(8,128)(2,1)} %block.1) | data formatting | bytes 1572864

commit v3 on v2

--- a/solution.py
+++ b/solution.py
@@ -110,23 +110,36 @@
         copy.start()
     tb, g1, s1, b1, g2, s2, b2 = (pv.at[n] for n in range(7))
 
-    total = jnp.int32(0)
-    for k in range(nf):
-        offs[k] = total
-        total = total + counts[k]
-
+    for i in range(2):
+        hr[i, frames:tp] = jnp.zeros((1, J, C), BF16)
+    pl.semaphore_wait(barrier, len(near))
+
+    rows_out = [
+        remote(video.at[:, 0], hr.at[1, 0:frames], p1_send.at[0], p1_recv.at[0], hup, f),
+        remote(video.at[:, 1], hr.at[0, 0:frames], p1_send.at[1], p1_recv.at[1], hdn, f),
+    ]
+    for copy in rows_out:
+        copy.start()
+
+    rings = ((0, on_z, nf), (1, on_y, ny), (2, on_x, nx))
+
+    def tell(reach):
+        for n, on, size in rings:
+            if reach < size // 2:
+                for step in (-reach, reach):
+                    greet(known.at[n, reach // 2], *on(step))
+
+    def hear(reach):
+        for n, on, size in rings:
+            if reach < size // 2:
+                pl.semaphore_wait(known.at[n, reach // 2], 2)
+
+    tell(1)
     zero8 = jnp.zeros((8, C), F32)
     gt[0:8, :] = zero8
     gt[8 + wide : 16 + wide, :] = zero8
-    g4[0:8, :] = zero8
-    g4[8 + width : 16 + width, :] = zero8
-    for a in range(3):
-        for i in range(2):
-            tc[a, i, 0:16, :] = jnp.zeros((16, C), F32)
-
     pick_left = one_hot(fr, wide, lambda r, c: c == r * J).astype(BF16)
     pick_right = one_hot(fr, wide, lambda r, c: c == r * J + J - 1).astype(BF16)
-
     copy_video.wait()
     for i in range(2):
         act = silu(vid[:, i].astype(F32)).astype(BF16)
@@ -136,11 +149,7 @@
         colb[0, i] = jnp.dot(pick_left, flat, preferred_element_type=F32).astype(BF16)
         colb[1, i] = jnp.dot(pick_right, flat, preferred_element_type=F32).astype(BF16)
 
-    pl.semaphore_wait(barrier, len(near))
-
     borders = [
-        (rowb.at[0], hr.at[1], hup, f),
-        (rowb.at[1], hr.at[0], hdn, f),
         (colb.at[0], hc.at[1, 1:3], h, fl),
         (colb.at[1], hc.at[0, 1:3], h, fr_),
         (colb.at[0, 0], hc.at[1, 3], hup, fl),
@@ -148,34 +157,24 @@
         (colb.at[0, 1], hc.at[1, 0], hdn, fl),
         (colb.at[1, 1], hc.at[0, 0], hdn, fr_),
     ]
-    p1 = [
-        remote(src, dst, p1_send.at[n], p1_recv.at[n], hh, ff)
+    cols_out = [
+        remote(src, dst, p1_send.at[2 + n], p1_recv.at[2 + n], hh, ff)
         for n, (src, dst, hh, ff) in enumerate(borders)
     ]
-    for copy in p1:
+    for copy in cols_out:
         copy.start()
-
-    rings = ((on_z, nf), (on_y, ny), (on_x, nx))
-    reach = 1
-    while reach < nf // 2:
-        for n, (on, size) in enumerate(rings):
-            if reach < size // 2:
-                for step in (-reach, reach):
-                    greet(known.at[n, reach // 2], *on(step))
-        for n, (on, size) in enumerate(rings):
-            if reach < size // 2:
-                pl.semaphore_wait(known.at[n, reach // 2], 2)
-        reach *= 2
-
-    for copy in p1:
-        copy.wait()
-
-    for copy in own_w:
-        copy.wait()
-    for i in range(2):
-        for s in range(1, ny):
-            here = wb.at[i, mine, :, lanes]
-            remote(here, here, wy_send.at[i], wy_recv.at[i], *on_y(s)).start()
+    hear(1)
+    tell(2)
+
+    total = jnp.int32(0)
+    for k in range(nf):
+        offs[k] = total
+        total = total + counts[k]
+    g4[0:8, :] = zero8
+    g4[8 + width : 16 + width, :] = zero8
+    for a in range(3):
+        for i in range(2):
+            tc[a, i, 0:16, :] = jnp.zeros((16, C), F32)
 
     put_left = one_hot(wide, fr, lambda r, c: r == c * J).astype(BF16)
     put_right = one_hot(wide, fr, lambda r, c: r == c * J + J - 1).astype(BF16)
@@ -184,10 +183,14 @@
     keep_right = jnp.where(f < nf - 1, 1.0, 0.0)
     keep_top = jnp.where(h > 0, 1.0, 0.0)
     keep_bottom = jnp.where(h < nh - 1, 1.0, 0.0)
-    for ip in range(4):
-        source = (hr.at[0], rowb.at[0], rowb.at[1], hr.at[1])[ip]
+
+    def bordered(ip):
         keep = (keep_top, 1.0, 1.0, keep_bottom)[ip]
-        middle = source[...].astype(F32).reshape(wide, C) * keep
+        if ip in (1, 2):
+            middle = rowb[ip - 1].astype(F32).reshape(wide, C)
+        else:
+            raw = hr[ip // 3].astype(F32).reshape(wide, C)
+            middle = silu(raw).astype(BF16).astype(F32) * keep
         gt[8 : 8 + wide, :] = middle
         lefts = jnp.dot(put_left, hc[0, ip], preferred_element_type=F32) * (keep * keep_left)
         rights = jnp.dot(put_right, hc[1, ip], preferred_element_type=F32) * (keep * keep_right)
@@ -195,24 +198,49 @@
         se[rows, 0:C] = jnp.where(col == 0, lefts, gt[7 : 7 + wide, :]).astype(BF16)
         se[rows, C : 2 * C] = middle.astype(BF16)
         se[rows, 2 * C : 3 * C] = jnp.where(col == J - 1, rights, gt[9 : 9 + wide, :]).astype(BF16)
+
+    def tap(a, i, b):
+        start = pl.multiple_of(a * (9 * C) + b * (3 * C), 3 * C)
+        return jnp.dot(
+            se[(i + b) * wide : (i + b + 1) * wide, :],
+            twv[pl.ds(start, 3 * C), :],
+            preferred_element_type=F32,
+        )
+
+    def own_taps(a, carry):
+        tc[a, 0, 16 : 16 + wide, :] = tap(a, 0, 1) + tap(a, 0, 2)
+        tc[a, 1, 16 : 16 + wide, :] = tap(a, 1, 0) + tap(a, 1, 1)
+        return carry
+
+    def border_taps(a, carry):
+        tc[a, 0, 16 : 16 + wide, :] += tap(a, 0, 0)
+        tc[a, 1, 16 : 16 + wide, :] += tap(a, 1, 2)
+        return carry
+
+    for copy in cols_out[:2]:
+        copy.wait()
+    bordered(1)
+    bordered(2)
+    hear(2)
+    tell(4)
+
+    for copy in own_w:
+        copy.wait()
+    for i in range(2):
+        for s in range(1, ny):
+            here = wb.at[i, mine, :, lanes]
+            remote(here, here, wy_send.at[i], wy_recv.at[i], *on_y(s)).start()
+
     copy_tw.wait()
     for copy in vectors:
         copy.wait()
-
-    def taps(a, carry):
-        for i in range(2):
-            acc = jnp.zeros((wide, C), F32)
-            for b in range(3):
-                start = pl.multiple_of(a * (9 * C) + b * (3 * C), 3 * C)
-                acc = acc + jnp.dot(
-                    se[(i + b) * wide : (i + b + 1) * wide, :],
-                    twv[pl.ds(start, 3 * C), :],
-                    preferred_element_type=F32,
-                )
-            tc[a, i, 16 : 16 + wide, :] = acc
-        return carry
-
-    lax.fori_loop(0, 3, taps, 0)
+    lax.fori_loop(0, 3, own_taps, 0)
+    for copy in rows_out + cols_out[2:]:
+        copy.wait()
+    bordered(0)
+    bordered(3)
+    lax.fori_loop(0, 3, border_taps, 0)
+    hear(4)
 
     n_all = frames * J
     sums = jnp.zeros((n_all, C), F32)
@@ -265,21 +293,53 @@
     for r in range(MOST):
         rec[r, :, f] = bs[my_offset + r]
 
-    block = pl.ds(x * (ny * su), ny * su)
-
-    def along_x(i):
-        await_bytes(wb.at[i, pl.ds(0, (ny - 1) * su), :, lanes], wy_recv.at[i])
-        for s in range(1, nx):
-            here = wb.at[i, block, :, lanes]
-            remote(here, here, wx_send.at[i], wx_recv.at[i], *on_x(s)).start()
+    size = ny * su
+    half = size // 2
+
+    def block(s):
+        return lax.rem(x + nx + s, nx) * size
+
+    def x_copy(i, start, count, sem, step):
+        here = wb.at[i, pl.ds(start, count), :, lanes]
+        remote(here, here, wx_send.at[i, sem], wx_recv.at[i, sem], *on_x(step)).start()
+
+    def x_await(i, count, sem, which):
+        await_bytes(wb.at[i, pl.ds(0, count), :, lanes], which.at[i, sem])
+
+    def both_first():
+        await_bytes(wb.at[0, pl.ds(0, (ny - 1) * su), :, lanes], wy_recv.at[0])
+        x_copy(0, block(0), size, 0, 1)
+        if nx > 2:
+            x_copy(0, block(0), size, 1, -1)
+
+    def both_second():
+        x_await(0, size, 0, wx_recv)
+        if nx > 2:
+            x_copy(0, block(-1), half, 2, 1)
+            x_await(0, size, 1, wx_recv)
+            x_copy(0, block(1) + half, half, 3, -1)
+
+    def both_last():
+        if nx > 2:
+            x_await(0, half, 2, wx_recv)
+            x_await(0, half, 3, wx_recv)
+
+    way = 1 - 2 * ((ny - y) // ny)
+
+    def one_way(n):
+        if n == 0:
+            await_bytes(wb.at[1, pl.ds(0, (ny - 1) * su), :, lanes], wy_recv.at[1])
+        else:
+            x_await(1, size, n - 1, wx_recv)
+        if n < nx - 1:
+            x_copy(1, block(-n * way), size, n, way)
 
     partner = f + 1 - 2 * core
     other = pl.ds(pl.multiple_of(128 - core * 128, 128), 128)
 
     def to_partner(i):
-        await_bytes(wb.at[i, pl.ds(0, (nx - 1) * ny * su), :, lanes], wx_recv.at[i])
-        half = wb.at[i, :, :, lanes]
-        remote(half, half, wp_send.at[i], wp_recv.at[i], h, partner).start()
+        mine_half = wb.at[i, :, :, lanes]
+        remote(mine_half, mine_half, wp_send.at[i], wp_recv.at[i], h, partner).start()
 
     def y_start(q, value):
         ysc[q, y] = value
@@ -329,15 +389,17 @@
         remote(rec.at[r, 0], ha.at[r, 1], ha_send.at[r, 0], ha_recv.at[r, 0], hup, f).start()
         remote(rec.at[r, 1], ha.at[r, 0], ha_send.at[r, 1], ha_recv.at[r, 1], hdn, f).start()
 
-    along_x(0)
+    both_first()
     await_bytes(rs.at[0 : nf - 1], st_recv)
     y_start(0, jnp.sum(rs[...], axis=0))
+    both_second()
     slot_in(0)
     x_start(0, y_finish(0))
-    along_x(1)
+    one_way(0)
     slot_in(1)
+    both_last()
+    to_partner(0)
     set_norm(0, x_finish(0), g1[...])
-    to_partner(0)
 
     keeps = (keep_top, None, None, keep_bottom)
 
@@ -413,16 +475,20 @@
         remote(first.at[r, 0], hb.at[r, 1], hb_send.at[r, 0], hb_recv.at[r, 0], hup, f).start()
         remote(first.at[r, 1], hb.at[r, 0], hb_send.at[r, 1], hb_recv.at[r, 1], hdn, f).start()
 
-        @pl.when(r == split - 1)
-        def _():
-            to_partner(1)
+        for n in range(1, nx - 1):
+
+            @pl.when(r == 2 * n - 1)
+            def _():
+                one_way(n)
 
         return carry
 
     lax.fori_loop(0, MOST, first_conv, 0)
+    one_way(nx - 1)
+    to_partner(1)
     x_start(1, y_finish(1))
+    x_start(2, y_finish(2))
     ready_weight(1)
-    x_start(2, y_finish(2))
     set_norm(1, x_finish(1), g2[...])
 
     my_count = counts[f]
@@ -445,8 +511,14 @@
 
     for i in range(2):
         await_bytes(wb.at[i, pl.ds(0, (ny - 1) * su), :, lanes], wy_send.at[i])
-        await_bytes(wb.at[i, pl.ds(0, (nx - 1) * ny * su), :, lanes], wx_send.at[i])
         await_bytes(wb.at[i, :, :, lanes], wp_send.at[i])
+    x_await(0, size, 0, wx_send)
+    if nx > 2:
+        x_await(0, size, 1, wx_send)
+        x_await(0, half, 2, wx_send)
+        x_await(0, half, 3, wx_send)
+    for n in range(nx - 1):
+        x_await(1, size, n, wx_send)
     await_bytes(sts.at[0 : nf - 1], st_send)
     await_bytes(stage.at[:, 0 : nf - 1], a2a_send)
     for q in range(3):
@@ -461,7 +533,7 @@
 
 def per_device(nf, nh, video, counts, tw, tb, g1, s1, w1, b1, g2, s2, w2, b2):
     frames = video.shape[0]
-    ny = 8 if nh % 8 == 0 else 2
+    ny = 8 if nh % 16 == 0 else 2
     nx = nh // ny
     su = w1.shape[0] // 8
     tp = frames + 1
@@ -505,7 +577,7 @@
         V((7, 1, C), F32),
         pltpu.SMEM((nf,), jnp.int32),
         dma((2,)), dma((8,)), dma((8,)), dma((2,)),
-        dma((2,)), dma((2,)), dma((2,)), dma((2,)), dma((2,)), dma((2,)),
+        dma((2,)), dma((2,)), dma((2, 4)), dma((2, 4)), dma((2,)), dma((2,)),
         dma, dma((MOST,)), dma, dma, dma((3,)), dma((3,)), dma((3,)), dma((3,)),
         dma((MOST, 2)), dma((MOST, 2)), dma((MOST, 2)), dma((MOST, 2)), dma((MOST,)), dma((7,)),
         pltpu.SemaphoreType.REGULAR((3, 3)),

time: 72.4 us -> 67.5 us (0.932)
  Pallas kernels: 69.5 us -> 65.2 us
    pallas_call x1, Pallas kernels: 69.5 us -> 65.2 us  [per_device(): pl.pallas_call(functools.partial(kernel, nf, nx, ny, frames, su, cells),...]
where the time goes in v3:
time: 67.5 us; the launch traced here: 67.3 us
  Pallas kernels  65.2 us (97%)
  local copies, waits for them, and re-layouts  2.06 us (3%)
    pallas_call x1, Pallas kernels, per_device(): pl.pallas_call(functools.partial(kernel, nf, nx, ny, frames, su, cells),...  65.2 us
    unnamed x1, local copies, waits for them, and re-layouts  2.06 us

profile of v3, /device:TPU:1, one launch (start us, length us, event | category | flops | bytes accessed | tf_op | source)
XLA Modules:
  0.0 67.3 jit_solution(5126049752190407632)
XLA Ops:
  0.0 65.2 %block.1 = bf16[6,2,128,256]{3,2,1,0:T(8,128)(2,1)} custom-call(s32[16]{0:T(128)} %counts.1, bf16[33,2,8,256]{3,2,1,0:T(8,128)(2,1)} %video.1, bf16[6912,256]{1,0:T(8,128)(2,1)} %tw.1, bf16[9,8,256]{2,1,0:T(8,128)(2,1)} %bitcast.9, bf16[9,8,256]{2,1,0:T(8,128)(2,1)} %bitcast.10, f32[1,256]{1,0:T(1,128)} %bitcast.11, f32[1,256]{1,0:T(1,128)} %bitcast.12, ...), custom_call_target="tpu_custom_call" | custom-call | tf_op jit(solution)/shard_map/block/pallas_call | solution.py:585
  65.3 2.1 %copy.14 = bf16[6,2,128,256]{3,2,1,0:T(8,128)(2,1)} copy(bf16[6,2,128,256]{3,2,1,0:T(8,128)(2,1)} %block.1) | data formatting | bytes 1572864

commit v4 on v3

--- a/solution.py
+++ b/solution.py
@@ -38,10 +38,10 @@
     counts, video, tw, w1, w2, tb_in, g1_in, s1_in, b1_in, g2_in, s2_in, b2_in,
     out,
     vid, twv, rowb, colb, hr, hc, gt, se, tc, bs, stage, sts, rs, ysc, xsc, fsb,
-    rec, ha, hb, first, g4, so, wb, wr, stat, mu, sc, outv, pv, offs,
+    rec, ha, first, g4, so, wb, wr, stat, mu, sc, outv, pv, offs,
     local_sem, p1_send, p1_recv, wl_sem, wy_send, wy_recv, wx_send, wx_recv, wp_send, wp_recv,
     a2a_send, a2a_recv, st_send, st_recv, y_send, y_recv, x_send, x_recv,
-    ha_send, ha_recv, hb_send, hb_recv, out_sem, pv_sem, known,
+    ha_send, ha_recv, out_sem, pv_sem, known,
 ):
     nh = nx * ny
     tp = frames + 1
@@ -386,14 +386,14 @@
 
     def slot_in(r):
         await_bytes(rec.at[r, :, 0 : nf - 1], a2a_recv.at[r])
-        remote(rec.at[r, 0], ha.at[r, 1], ha_send.at[r, 0], ha_recv.at[r, 0], hup, f).start()
-        remote(rec.at[r, 1], ha.at[r, 0], ha_send.at[r, 1], ha_recv.at[r, 1], hdn, f).start()
+        remote(rec.at[r], ha.at[r, 1], ha_send.at[r, 0], ha_recv.at[r, 0], hup, f).start()
+        remote(rec.at[r], ha.at[r, 0], ha_send.at[r, 1], ha_recv.at[r, 1], hdn, f).start()
 
     both_first()
     await_bytes(rs.at[0 : nf - 1], st_recv)
     y_start(0, jnp.sum(rs[...], axis=0))
+    slot_in(0)
     both_second()
-    slot_in(0)
     x_start(0, y_finish(0))
     one_way(0)
     slot_in(1)
@@ -401,13 +401,12 @@
     to_partner(0)
     set_norm(0, x_finish(0), g1[...])
 
-    keeps = (keep_top, None, None, keep_bottom)
-
-    def convolve(r, rows_of, q, shift, weight):
+    def convolve(r, fields, keeps, q, shift, weight):
         mean = mu[q, pl.ds(r, 1), :]
         scale = sc[q, pl.ds(r, 1), :]
-        for ip in range(4):
-            normed = silu((rows_of(ip) - mean) * scale + shift)
+        for ip, field in enumerate(fields):
+            value = field[...].astype(F32).reshape(width, C)
+            normed = silu((value - mean) * scale + shift)
             if keeps[ip] is not None:
                 normed = normed * keeps[ip]
             g4[8 : 8 + width, :] = normed
@@ -415,28 +414,17 @@
             so[rows, 0:C] = g4[7 : 7 + width, :].astype(BF16)
             so[rows, C : 2 * C] = normed.astype(BF16)
             so[rows, 2 * C : 3 * C] = g4[9 : 9 + width, :].astype(BF16)
-        acc = jnp.zeros((2 * width, C), F32)
-        for b in range(3):
-            acc = acc + jnp.dot(
-                so[b * width : (b + 2) * width, :],
-                wr[weight, b * 3 * C : (b + 1) * 3 * C, :],
-                preferred_element_type=F32,
-            )
-        return acc
-
-    def first_rows(r):
-        def get(ip):
-            ref = (ha.at[r, 0], rec.at[r, 0], rec.at[r, 1], ha.at[r, 1])[ip]
-            return ref[...].astype(F32).reshape(width, C)
-
-        return get
-
-    def second_rows(r):
-        def get(ip):
-            ref = (hb.at[r, 0], first.at[r, 0], first.at[r, 1], hb.at[r, 1])[ip]
-            return ref[...].astype(F32)
-
-        return get
+        pairs = []
+        for top in range(0, len(fields) - 2, 2):
+            acc = jnp.zeros((2 * width, C), F32)
+            for b in range(3):
+                acc = acc + jnp.dot(
+                    so[(top + b) * width : (top + b + 2) * width, :],
+                    wr[weight, b * 3 * C : (b + 1) * 3 * C, :],
+                    preferred_element_type=F32,
+                )
+            pairs.append(acc)
+        return pairs
 
     stat[...] = jnp.zeros_like(stat)
     split = MOST - 2
@@ -455,10 +443,15 @@
 
         await_bytes(ha.at[r, 0], ha_recv.at[r, 0])
         await_bytes(ha.at[r, 1], ha_recv.at[r, 1])
-        result = convolve(r, first_rows(r), 0, s1[...], 0) + b1[...]
-        first[r, 0] = result[0:width].astype(BF16)
-        first[r, 1] = result[width : 2 * width].astype(BF16)
-        rounded = first[r, 0].astype(F32), first[r, 1].astype(F32)
+        fields = (
+            ha.at[r, 0, 0], ha.at[r, 0, 1], rec.at[r, 0], rec.at[r, 1], ha.at[r, 1, 0], ha.at[r, 1, 1],
+        )
+        keeps = (keep_top, keep_top, None, None, keep_bottom, keep_bottom)
+        for n, pair in enumerate(convolve(r, fields, keeps, 0, s1[...], 0)):
+            pair = pair + b1[...]
+            first[r, 2 * n] = pair[0:width].astype(BF16)
+            first[r, 2 * n + 1] = pair[width : 2 * width].astype(BF16)
+        rounded = first[r, 1].astype(F32), first[r, 2].astype(F32)
         sums = rounded[0] + rounded[1]
         squares = rounded[0] * rounded[0] + rounded[1] * rounded[1]
         stat[0, pl.ds(r, 1), :] = jnp.sum(sums, axis=0, keepdims=True)
@@ -471,9 +464,6 @@
         @pl.when(r == MOST - 1)
         def _():
             sums_start(2)
-
-        remote(first.at[r, 0], hb.at[r, 1], hb_send.at[r, 0], hb_recv.at[r, 0], hup, f).start()
-        remote(first.at[r, 1], hb.at[r, 0], hb_send.at[r, 1], hb_recv.at[r, 1], hdn, f).start()
 
         for n in range(1, nx - 1):
 
@@ -494,9 +484,9 @@
     my_count = counts[f]
 
     def second_conv(q, r, carry):
-        await_bytes(hb.at[r, 0], hb_recv.at[r, 0])
-        await_bytes(hb.at[r, 1], hb_recv.at[r, 1])
-        result = convolve(r, second_rows(r), q, s2[...], 1) + b2[...]
+        fields = tuple(first.at[r, n] for n in range(4))
+        keeps = (keep_top, None, None, keep_bottom)
+        result = convolve(r, fields, keeps, q, s2[...], 1)[0] + b2[...]
         live = r < my_count
         for i in range(2):
             kept = rec[r, i].astype(F32).reshape(width, C)
@@ -526,8 +516,7 @@
         await_bytes(xsc.at[q, 0 : nx - 1], x_send.at[q])
     for r in range(MOST):
         for i in range(2):
-            await_bytes(rec.at[r, i], ha_send.at[r, i])
-            await_bytes(first.at[r, i], hb_send.at[r, i])
+            await_bytes(rec.at[r], ha_send.at[r, i])
         pltpu.make_async_copy(outv.at[r], out.at[r], out_sem.at[r]).wait()
 
 
@@ -563,11 +552,10 @@
         V((3, nx, 8, SUM_LANES), F32),
         V((fr, SUM_LANES), F32),
         V((MOST, 2, nf, J, C), BF16),
-        V((MOST, 2, nf, J, C), BF16),
-        V((MOST, 2, width, C), BF16),
-        V((MOST, 2, width, C), BF16),
+        V((MOST, 2, 2, nf, J, C), BF16),
+        V((MOST, 4, width, C), BF16),
         V((width + 16, C), F32),
-        V((4 * width, 3 * C), BF16),
+        V((6 * width, 3 * C), BF16),
         V((2, nh * su, 8, C), BF16),
         V((2, 9 * C, C), BF16),
         V((2, 8, C), F32),
@@ -579,7 +567,7 @@
         dma((2,)), dma((8,)), dma((8,)), dma((2,)),
         dma((2,)), dma((2,)), dma((2, 4)), dma((2, 4)), dma((2,)), dma((2,)),
         dma, dma((MOST,)), dma, dma, dma((3,)), dma((3,)), dma((3,)), dma((3,)),
-        dma((MOST, 2)), dma((MOST, 2)), dma((MOST, 2)), dma((MOST, 2)), dma((MOST,)), dma((7,)),
+        dma((MOST, 2)), dma((MOST, 2)), dma((MOST,)), dma((7,)),
         pltpu.SemaphoreType.REGULAR((3, 3)),
     ]
     return pl.pallas_call(

time: 67.5 us -> 76.1 us (1.13)
  the two profiles are of different devices: /device:TPU:1 before, /device:TPU:128 now
where the time goes in v4:
time: 76.1 us; the launch traced here: 75.9 us
  Pallas kernels  73.9 us (97%)
  local copies, waits for them, and re-layouts  2.06 us (3%)
    pallas_call x1, Pallas kernels, per_device(): pl.pallas_call(functools.partial(kernel, nf, nx, ny, frames, su, cells),...  73.9 us
    unnamed x1, local copies, waits for them, and re-layouts  2.06 us

profile of v4, /device:TPU:128, one launch (start us, length us, event | category | flops | bytes accessed | tf_op | source)
XLA Modules:
  0.0 75.9 jit_solution(8457268022009603578)
XLA Ops:
  0.0 73.9 %block.1 = bf16[6,2,128,256]{3,2,1,0:T(8,128)(2,1)} custom-call(s32[16]{0:T(128)} %counts.1, bf16[33,2,8,256]{3,2,1,0:T(8,128)(2,1)} %video.1, bf16[6912,256]{1,0:T(8,128)(2,1)} %tw.1, bf16[9,8,256]{2,1,0:T(8,128)(2,1)} %bitcast.9, bf16[9,8,256]{2,1,0:T(8,128)(2,1)} %bitcast.10, f32[1,256]{1,0:T(1,128)} %bitcast.11, f32[1,256]{1,0:T(1,128)} %bitcast.12, ...), custom_call_target="tpu_custom_call" | custom-call | tf_op jit(solution)/shard_map/block/pallas_call | solution.py:573
  73.9 2.1 %copy.14 = bf16[6,2,128,256]{3,2,1,0:T(8,128)(2,1)} copy(bf16[6,2,128,256]{3,2,1,0:T(8,128)(2,1)} %block.1) | data formatting | bytes 1572864

commit v5 on v3

--- a/solution.py
+++ b/solution.py
@@ -33,13 +33,17 @@
     return jnp.where(fn(r, c), 1.0, 0.0).astype(F32)
 
 
+def size_y(nh):
+    return 8 if nh % 16 == 0 else 2
+
+
 def kernel(
     nf, nx, ny, frames, su, cells,
     counts, video, tw, w1, w2, tb_in, g1_in, s1_in, b1_in, g2_in, s2_in, b2_in,
     out,
     vid, twv, rowb, colb, hr, hc, gt, se, tc, bs, stage, sts, rs, ysc, xsc, fsb,
     rec, ha, hb, first, g4, so, wb, wr, stat, mu, sc, outv, pv, offs,
-    local_sem, p1_send, p1_recv, wl_sem, wy_send, wy_recv, wx_send, wx_recv, wp_send, wp_recv,
+    local_sem, p1_send, p1_recv, wl_sem, ring_send, ring_recv, wy_send, wy_recv, wx_send, wx_recv, wp_send, wp_recv,
     a2a_send, a2a_recv, st_send, st_recv, y_send, y_recv, x_send, x_recv,
     ha_send, ha_recv, hb_send, hb_recv, out_sem, pv_sem, known,
 ):
@@ -94,9 +98,15 @@
     copy_tw.start()
     lane0 = pl.multiple_of(core * 128, 128)
     lanes = pl.ds(lane0, 128)
-    mine = pl.ds(h * su, su)
+
+    def shards_at(i, yy):
+        return wb.at[i, :, pl.ds(yy * su, su), :, lanes]
+
+    def own_shard(i):
+        return wb.at[i, x, pl.ds(y * su, su), :, lanes]
+
     own_w = [
-        pltpu.make_async_copy(w.at[:, :, lanes], wb.at[i, mine, :, lanes], wl_sem.at[i])
+        pltpu.make_async_copy(w.at[:, :, lanes], own_shard(i), wl_sem.at[i])
         for i, w in enumerate((w1, w2))
     ]
     for copy in own_w:
@@ -166,6 +176,23 @@
     hear(1)
     tell(2)
 
+    own_w[0].wait()
+    for s in range(1, nx):
+        remote(own_shard(0), own_shard(0), wx_send.at[0, 0], wx_recv.at[0, 0], *on_x(s)).start()
+    plus, minus = ny // 2, ny - 1 - ny // 2
+    others_x = wb.at[0, 0 : nx - 1, pl.ds(0, su), :, lanes]
+
+    def ring(k):
+        if k == 0:
+            await_bytes(others_x, wx_recv.at[0, 0])
+        for d, count, step in ((0, plus, 1), (1, minus, -1)):
+            if 0 <= k - 1 < count:
+                await_bytes(shards_at(0, 0), ring_recv.at[d, k - 1])
+            if k < count:
+                here = shards_at(0, lax.rem(y + ny - step * k, ny))
+                remote(here, here, ring_send.at[d, k], ring_recv.at[d, k], *on_y(step)).start()
+
+
     total = jnp.int32(0)
     for k in range(nf):
         offs[k] = total
@@ -224,13 +251,7 @@
     hear(2)
     tell(4)
 
-    for copy in own_w:
-        copy.wait()
-    for i in range(2):
-        for s in range(1, ny):
-            here = wb.at[i, mine, :, lanes]
-            remote(here, here, wy_send.at[i], wy_recv.at[i], *on_y(s)).start()
-
+    ring(0)
     copy_tw.wait()
     for copy in vectors:
         copy.wait()
@@ -240,6 +261,12 @@
     bordered(0)
     bordered(3)
     lax.fori_loop(0, 3, border_taps, 0)
+    ring(1)
+
+    own_w[1].wait()
+    for s in range(1, ny):
+        remote(own_shard(1), own_shard(1), wy_send, wy_recv, *on_y(s)).start()
+
     hear(4)
 
     n_all = frames * J
@@ -293,52 +320,22 @@
     for r in range(MOST):
         rec[r, :, f] = bs[my_offset + r]
 
-    size = ny * su
-    half = size // 2
-
-    def block(s):
-        return lax.rem(x + nx + s, nx) * size
-
-    def x_copy(i, start, count, sem, step):
-        here = wb.at[i, pl.ds(start, count), :, lanes]
-        remote(here, here, wx_send.at[i, sem], wx_recv.at[i, sem], *on_x(step)).start()
-
-    def x_await(i, count, sem, which):
-        await_bytes(wb.at[i, pl.ds(0, count), :, lanes], which.at[i, sem])
-
-    def both_first():
-        await_bytes(wb.at[0, pl.ds(0, (ny - 1) * su), :, lanes], wy_recv.at[0])
-        x_copy(0, block(0), size, 0, 1)
-        if nx > 2:
-            x_copy(0, block(0), size, 1, -1)
-
-    def both_second():
-        x_await(0, size, 0, wx_recv)
-        if nx > 2:
-            x_copy(0, block(-1), half, 2, 1)
-            x_await(0, size, 1, wx_recv)
-            x_copy(0, block(1) + half, half, 3, -1)
-
-    def both_last():
-        if nx > 2:
-            x_await(0, half, 2, wx_recv)
-            x_await(0, half, 3, wx_recv)
-
     way = 1 - 2 * ((ny - y) // ny)
 
     def one_way(n):
         if n == 0:
-            await_bytes(wb.at[1, pl.ds(0, (ny - 1) * su), :, lanes], wy_recv.at[1])
+            await_bytes(wb.at[1, 0, pl.ds(0, (ny - 1) * su), :, lanes], wy_recv)
         else:
-            x_await(1, size, n - 1, wx_recv)
+            await_bytes(wb.at[1, 0, :, :, lanes], wx_recv.at[1, n - 1])
         if n < nx - 1:
-            x_copy(1, block(-n * way), size, n, way)
+            here = wb.at[1, lax.rem(x + nx - n * way + nx, nx), :, :, lanes]
+            remote(here, here, wx_send.at[1, n], wx_recv.at[1, n], *on_x(way)).start()
 
     partner = f + 1 - 2 * core
     other = pl.ds(pl.multiple_of(128 - core * 128, 128), 128)
 
     def to_partner(i):
-        mine_half = wb.at[i, :, :, lanes]
+        mine_half = wb.at[i, :, :, :, lanes]
         remote(mine_half, mine_half, wp_send.at[i], wp_recv.at[i], h, partner).start()
 
     def y_start(q, value):
@@ -374,11 +371,13 @@
         sc[q] = lax.rsqrt(jnp.maximum(var, 0.0) + 1e-06) * gain
 
     def ready_weight(i):
-        await_bytes(wb.at[i, :, :, other], wp_recv.at[i])
+        await_bytes(wb.at[i, :, :, :, other], wp_recv.at[i])
         step = 18
+        steps = ny * su // step
 
         def widen(n, carry):
-            rows = wb[i, pl.ds(n * step, step)].astype(F32).reshape(step * 8, C)
+            rows = wb[i, n // steps, pl.ds(lax.rem(n, steps) * step, step)]
+            rows = rows.astype(F32).reshape(step * 8, C)
             wr[i, pl.ds(pl.multiple_of(n * step * 8, step * 8), step * 8), :] = rows.astype(BF16)
             return carry
 
@@ -389,16 +388,16 @@
         remote(rec.at[r, 0], ha.at[r, 1], ha_send.at[r, 0], ha_recv.at[r, 0], hup, f).start()
         remote(rec.at[r, 1], ha.at[r, 0], ha_send.at[r, 1], ha_recv.at[r, 1], hdn, f).start()
 
-    both_first()
+    ring(2)
     await_bytes(rs.at[0 : nf - 1], st_recv)
     y_start(0, jnp.sum(rs[...], axis=0))
-    both_second()
+    ring(3)
     slot_in(0)
+    ring(4)
+    to_partner(0)
     x_start(0, y_finish(0))
     one_way(0)
     slot_in(1)
-    both_last()
-    to_partner(0)
     set_norm(0, x_finish(0), g1[...])
 
     keeps = (keep_top, None, None, keep_bottom)
@@ -509,16 +508,15 @@
     set_norm(2, x_finish(2), g2[...])
     lax.fori_loop(split, MOST, functools.partial(second_conv, 2), 0)
 
+    await_bytes(others_x, wx_send.at[0, 0])
+    for d, count in ((0, plus), (1, minus)):
+        for k in range(count):
+            await_bytes(shards_at(0, 0), ring_send.at[d, k])
+    await_bytes(wb.at[1, 0, pl.ds(0, (ny - 1) * su), :, lanes], wy_send)
+    for n in range(nx - 1):
+        await_bytes(wb.at[1, 0, :, :, lanes], wx_send.at[1, n])
     for i in range(2):
-        await_bytes(wb.at[i, pl.ds(0, (ny - 1) * su), :, lanes], wy_send.at[i])
-        await_bytes(wb.at[i, :, :, lanes], wp_send.at[i])
-    x_await(0, size, 0, wx_send)
-    if nx > 2:
-        x_await(0, size, 1, wx_send)
-        x_await(0, half, 2, wx_send)
-        x_await(0, half, 3, wx_send)
-    for n in range(nx - 1):
-        x_await(1, size, n, wx_send)
+        await_bytes(wb.at[i, :, :, :, lanes], wp_send.at[i])
     await_bytes(sts.at[0 : nf - 1], st_send)
     await_bytes(stage.at[:, 0 : nf - 1], a2a_send)
     for q in range(3):
@@ -533,7 +531,7 @@
 
 def per_device(nf, nh, video, counts, tw, tb, g1, s1, w1, b1, g2, s2, w2, b2):
     frames = video.shape[0]
-    ny = 8 if nh % 16 == 0 else 2
+    ny = size_y(nh)
     nx = nh // ny
     su = w1.shape[0] // 8
     tp = frames + 1
@@ -568,7 +566,7 @@
         V((MOST, 2, width, C), BF16),
         V((width + 16, C), F32),
         V((4 * width, 3 * C), BF16),
-        V((2, nh * su, 8, C), BF16),
+        V((2, nx, ny * su, 8, C), BF16),
         V((2, 9 * C, C), BF16),
         V((2, 8, C), F32),
         V((3, 8, C), F32),
@@ -577,7 +575,7 @@
         V((7, 1, C), F32),
         pltpu.SMEM((nf,), jnp.int32),
         dma((2,)), dma((8,)), dma((8,)), dma((2,)),
-        dma((2,)), dma((2,)), dma((2, 4)), dma((2, 4)), dma((2,)), dma((2,)),
+        dma((2, 4)), dma((2, 4)), dma, dma, dma((2, 4)), dma((2, 4)), dma((2,)), dma((2,)),
         dma, dma((MOST,)), dma, dma, dma((3,)), dma((3,)), dma((3,)), dma((3,)),
         dma((MOST, 2)), dma((MOST, 2)), dma((MOST, 2)), dma((MOST, 2)), dma((MOST,)), dma((7,)),
         pltpu.SemaphoreType.REGULAR((3, 3)),

time: 67.5 us -> 68.5 us (1.015)
  no operation moved by 1% of the time
where the time goes in v5:
time: 68.5 us; the launch traced here: 67.9 us
  Pallas kernels  65.8 us (96%)
  local copies, waits for them, and re-layouts  2.06 us (3%)
    pallas_call x1, Pallas kernels, per_device(): pl.pallas_call(functools.partial(kernel, nf, nx, ny, frames, su, cells),...  65.8 us
    unnamed x1, local copies, waits for them, and re-layouts  2.06 us

profile of v5, /device:TPU:1, one launch (start us, length us, event | category | flops | bytes accessed | tf_op | source)
XLA Modules:
  0.0 67.9 jit_solution(14507022621025616244)
XLA Ops:
  0.0 65.8 %block.1 = bf16[6,2,128,256]{3,2,1,0:T(8,128)(2,1)} custom-call(s32[16]{0:T(128)} %counts.1, bf16[33,2,8,256]{3,2,1,0:T(8,128)(2,1)} %video.1, bf16[6912,256]{1,0:T(8,128)(2,1)} %tw.1, bf16[9,8,256]{2,1,0:T(8,128)(2,1)} %bitcast.9, bf16[9,8,256]{2,1,0:T(8,128)(2,1)} %bitcast.10, f32[1,256]{1,0:T(1,128)} %bitcast.11, f32[1,256]{1,0:T(1,128)} %bitcast.12, ...), custom_call_target="tpu_custom_call" | custom-call | tf_op jit(solution)/shard_map/block/pallas_call | solution.py:583
  65.8 2.1 %copy.14 = bf16[6,2,128,256]{3,2,1,0:T(8,128)(2,1)} copy(bf16[6,2,128,256]{3,2,1,0:T(8,128)(2,1)} %block.1) | data formatting | bytes 1572864

commit v6 on v3

--- a/solution.py
+++ b/solution.py
@@ -306,11 +306,19 @@
     def x_await(i, count, sem, which):
         await_bytes(wb.at[i, pl.ds(0, count), :, lanes], which.at[i, sem])
 
+    partner = f + 1 - 2 * core
+    other = pl.ds(pl.multiple_of(128 - core * 128, 128), 128)
+
+    def to_partner(i, start, count):
+        here = wb.at[i, pl.ds(start, count), :, lanes]
+        remote(here, here, wp_send.at[i], wp_recv.at[i], h, partner).start()
+
     def both_first():
         await_bytes(wb.at[0, pl.ds(0, (ny - 1) * su), :, lanes], wy_recv.at[0])
         x_copy(0, block(0), size, 0, 1)
         if nx > 2:
             x_copy(0, block(0), size, 1, -1)
+        to_partner(0, block(0), size)
 
     def both_second():
         x_await(0, size, 0, wx_recv)
@@ -318,11 +326,14 @@
             x_copy(0, block(-1), half, 2, 1)
             x_await(0, size, 1, wx_recv)
             x_copy(0, block(1) + half, half, 3, -1)
+            to_partner(0, block(-1), size)
+        to_partner(0, block(1), size)
 
     def both_last():
         if nx > 2:
             x_await(0, half, 2, wx_recv)
             x_await(0, half, 3, wx_recv)
+            to_partner(0, block(2), size)
 
     way = 1 - 2 * ((ny - y) // ny)
 
@@ -333,13 +344,6 @@
             x_await(1, size, n - 1, wx_recv)
         if n < nx - 1:
             x_copy(1, block(-n * way), size, n, way)
-
-    partner = f + 1 - 2 * core
-    other = pl.ds(pl.multiple_of(128 - core * 128, 128), 128)
-
-    def to_partner(i):
-        mine_half = wb.at[i, :, :, lanes]
-        remote(mine_half, mine_half, wp_send.at[i], wp_recv.at[i], h, partner).start()
 
     def y_start(q, value):
         ysc[q, y] = value
@@ -398,7 +402,6 @@
     one_way(0)
     slot_in(1)
     both_last()
-    to_partner(0)
     set_norm(0, x_finish(0), g1[...])
 
     keeps = (keep_top, None, None, keep_bottom)
@@ -441,6 +444,10 @@
     stat[...] = jnp.zeros_like(stat)
     split = MOST - 2
 
+    def send_first(r):
+        remote(first.at[r, 0], hb.at[r, 1], hb_send.at[r, 0], hb_recv.at[r, 0], hup, f).start()
+        remote(first.at[r, 1], hb.at[r, 0], hb_send.at[r, 1], hb_recv.at[r, 1], hdn, f).start()
+
     def sums_start(q):
         y_start(q, hdot(stat[0], sum_map) + hdot(stat[1], sq_map))
 
@@ -472,8 +479,9 @@
         def _():
             sums_start(2)
 
-        remote(first.at[r, 0], hb.at[r, 1], hb_send.at[r, 0], hb_recv.at[r, 0], hup, f).start()
-        remote(first.at[r, 1], hb.at[r, 0], hb_send.at[r, 1], hb_recv.at[r, 1], hdn, f).start()
+        @pl.when(r < MOST - 1)
+        def _():
+            send_first(r)
 
         for n in range(1, nx - 1):
 
@@ -484,12 +492,11 @@
         return carry
 
     lax.fori_loop(0, MOST, first_conv, 0)
+    x_start(1, y_finish(1))
     one_way(nx - 1)
-    to_partner(1)
-    x_start(1, y_finish(1))
-    x_start(2, y_finish(2))
+    to_partner(1, 0, nx * size)
+    set_norm(1, x_finish(1), g2[...])
     ready_weight(1)
-    set_norm(1, x_finish(1), g2[...])
 
     my_count = counts[f]
 
@@ -505,7 +512,10 @@
         pltpu.make_async_copy(outv.at[r], out.at[r], out_sem.at[r]).start()
         return carry
 
-    lax.fori_loop(0, split, functools.partial(second_conv, 1), 0)
+    lax.fori_loop(0, 1, functools.partial(second_conv, 1), 0)
+    x_start(2, y_finish(2))
+    send_first(MOST - 1)
+    lax.fori_loop(1, split, functools.partial(second_conv, 1), 0)
     set_norm(2, x_finish(2), g2[...])
     lax.fori_loop(split, MOST, functools.partial(second_conv, 2), 0)
 

time: 67.5 us -> 67.7 us (level)
  no operation moved by 1% of the time
where the time goes in v6:
time: 67.7 us; the launch traced here: 67.4 us
  Pallas kernels  65.3 us (96%)
  local copies, waits for them, and re-layouts  2.06 us (3%)
    pallas_call x1, Pallas kernels, per_device(): pl.pallas_call(functools.partial(kernel, nf, nx, ny, frames, su, cells),...  65.3 us
    unnamed x1, local copies, waits for them, and re-layouts  2.06 us

profile of v6, /device:TPU:1, one launch (start us, length us, event | category | flops | bytes accessed | tf_op | source)
XLA Modules:
  0.0 67.4 jit_solution(16500666172269952440)
XLA Ops:
  0.0 65.3 %block.1 = bf16[6,2,128,256]{3,2,1,0:T(8,128)(2,1)} custom-call(s32[16]{0:T(128)} %counts.1, bf16[33,2,8,256]{3,2,1,0:T(8,128)(2,1)} %video.1, bf16[6912,256]{1,0:T(8,128)(2,1)} %tw.1, bf16[9,8,256]{2,1,0:T(8,128)(2,1)} %bitcast.9, bf16[9,8,256]{2,1,0:T(8,128)(2,1)} %bitcast.10, f32[1,256]{1,0:T(1,128)} %bitcast.11, f32[1,256]{1,0:T(1,128)} %bitcast.12, ...), custom_call_target="tpu_custom_call" | custom-call | tf_op jit(solution)/shard_map/block/pallas_call | solution.py:595
  65.3 2.1 %copy.14 = bf16[6,2,128,256]{3,2,1,0:T(8,128)(2,1)} copy(bf16[6,2,128,256]{3,2,1,0:T(8,128)(2,1)} %block.1) | data formatting | bytes 1572864

commit v7 on v4

--- a/solution.py
+++ b/solution.py
@@ -16,6 +16,7 @@
 HIGH = lax.Precision.HIGHEST
 MESH = pl.DeviceIdType.MESH
 SUM_LANES = 128
+EARLY = 2
 
 
 def silu(v):
@@ -41,7 +42,7 @@
     rec, ha, first, g4, so, wb, wr, stat, mu, sc, outv, pv, offs,
     local_sem, p1_send, p1_recv, wl_sem, wy_send, wy_recv, wx_send, wx_recv, wp_send, wp_recv,
     a2a_send, a2a_recv, st_send, st_recv, y_send, y_recv, x_send, x_recv,
-    ha_send, ha_recv, out_sem, pv_sem, known,
+    ha_send, ha_recv, hb_send, hb_recv, out_sem, pv_sem, known,
 ):
     nh = nx * ny
     tp = frames + 1
@@ -306,11 +307,19 @@
     def x_await(i, count, sem, which):
         await_bytes(wb.at[i, pl.ds(0, count), :, lanes], which.at[i, sem])
 
+    partner = f + 1 - 2 * core
+    other = pl.ds(pl.multiple_of(128 - core * 128, 128), 128)
+
+    def to_partner(i, start, count):
+        here = wb.at[i, pl.ds(start, count), :, lanes]
+        remote(here, here, wp_send.at[i], wp_recv.at[i], h, partner).start()
+
     def both_first():
         await_bytes(wb.at[0, pl.ds(0, (ny - 1) * su), :, lanes], wy_recv.at[0])
         x_copy(0, block(0), size, 0, 1)
         if nx > 2:
             x_copy(0, block(0), size, 1, -1)
+        to_partner(0, block(0), size)
 
     def both_second():
         x_await(0, size, 0, wx_recv)
@@ -318,11 +327,14 @@
             x_copy(0, block(-1), half, 2, 1)
             x_await(0, size, 1, wx_recv)
             x_copy(0, block(1) + half, half, 3, -1)
+            to_partner(0, block(-1), size)
+        to_partner(0, block(1), size)
 
     def both_last():
         if nx > 2:
             x_await(0, half, 2, wx_recv)
             x_await(0, half, 3, wx_recv)
+            to_partner(0, block(2), size)
 
     way = 1 - 2 * ((ny - y) // ny)
 
@@ -334,13 +346,6 @@
         if n < nx - 1:
             x_copy(1, block(-n * way), size, n, way)
 
-    partner = f + 1 - 2 * core
-    other = pl.ds(pl.multiple_of(128 - core * 128, 128), 128)
-
-    def to_partner(i):
-        mine_half = wb.at[i, :, :, lanes]
-        remote(mine_half, mine_half, wp_send.at[i], wp_recv.at[i], h, partner).start()
-
     def y_start(q, value):
         ysc[q, y] = value
         for s in range(1, ny):
@@ -384,21 +389,24 @@
 
         lax.fori_loop(0, nh * su // step, widen, 0)
 
-    def slot_in(r):
+    def slot_in(r, early):
         await_bytes(rec.at[r, :, 0 : nf - 1], a2a_recv.at[r])
-        remote(rec.at[r], ha.at[r, 1], ha_send.at[r, 0], ha_recv.at[r, 0], hup, f).start()
-        remote(rec.at[r], ha.at[r, 0], ha_send.at[r, 1], ha_recv.at[r, 1], hdn, f).start()
+        if early:
+            pairs = (rec.at[r], ha.at[r, 1]), (rec.at[r], ha.at[r, 0])
+        else:
+            pairs = (rec.at[r, 0], ha.at[r, 1, 0]), (rec.at[r, 1], ha.at[r, 0, 1])
+        for n, ((src, dst), hh) in enumerate(zip(pairs, (hup, hdn))):
+            remote(src, dst, ha_send.at[r, n], ha_recv.at[r, n], hh, f).start()
 
     both_first()
     await_bytes(rs.at[0 : nf - 1], st_recv)
     y_start(0, jnp.sum(rs[...], axis=0))
-    slot_in(0)
     both_second()
+    slot_in(0, True)
     x_start(0, y_finish(0))
     one_way(0)
-    slot_in(1)
+    slot_in(1, True)
     both_last()
-    to_partner(0)
     set_norm(0, x_finish(0), g1[...])
 
     def convolve(r, fields, keeps, q, shift, weight):
@@ -429,28 +437,35 @@
     stat[...] = jnp.zeros_like(stat)
     split = MOST - 2
 
+    def send_first(r):
+        up, down = first.at[r, 1], first.at[r, 2]
+        remote(up, first.at[r, 3], hb_send.at[r, 0], hb_recv.at[r, 0], hup, f).start()
+        remote(down, first.at[r, 0], hb_send.at[r, 1], hb_recv.at[r, 1], hdn, f).start()
+
     def sums_start(q):
         y_start(q, hdot(stat[0], sum_map) + hdot(stat[1], sq_map))
 
-    def first_conv(r, carry):
+    def first_conv(early, r, carry):
         @pl.when(r + 2 < MOST)
         def _():
-            slot_in(r + 2)
-
-        @pl.when(r == 0)
-        def _():
-            ready_weight(0)
-
-        await_bytes(ha.at[r, 0], ha_recv.at[r, 0])
-        await_bytes(ha.at[r, 1], ha_recv.at[r, 1])
-        fields = (
-            ha.at[r, 0, 0], ha.at[r, 0, 1], rec.at[r, 0], rec.at[r, 1], ha.at[r, 1, 0], ha.at[r, 1, 1],
-        )
-        keeps = (keep_top, keep_top, None, None, keep_bottom, keep_bottom)
+            slot_in(r + 2, False)
+
+        above = ha.at[r, 0] if early else ha.at[r, 0, 1]
+        below = ha.at[r, 1] if early else ha.at[r, 1, 0]
+        await_bytes(below, ha_recv.at[r, 0])
+        await_bytes(above, ha_recv.at[r, 1])
+        own = (rec.at[r, 0], rec.at[r, 1])
+        if early:
+            fields = (above.at[0], above.at[1]) + own + (below.at[0], below.at[1])
+            keeps = (keep_top, keep_top, None, None, keep_bottom, keep_bottom)
+        else:
+            fields = (above,) + own + (below,)
+            keeps = (keep_top, None, None, keep_bottom)
+        place = 0 if early else 1
         for n, pair in enumerate(convolve(r, fields, keeps, 0, s1[...], 0)):
             pair = pair + b1[...]
-            first[r, 2 * n] = pair[0:width].astype(BF16)
-            first[r, 2 * n + 1] = pair[width : 2 * width].astype(BF16)
+            first[r, place + 2 * n] = pair[0:width].astype(BF16)
+            first[r, place + 2 * n + 1] = pair[width : 2 * width].astype(BF16)
         rounded = first[r, 1].astype(F32), first[r, 2].astype(F32)
         sums = rounded[0] + rounded[1]
         squares = rounded[0] * rounded[0] + rounded[1] * rounded[1]
@@ -465,6 +480,12 @@
         def _():
             sums_start(2)
 
+        if not early:
+
+            @pl.when(r < MOST - 1)
+            def _():
+                send_first(r)
+
         for n in range(1, nx - 1):
 
             @pl.when(r == 2 * n - 1)
@@ -473,17 +494,24 @@
 
         return carry
 
-    lax.fori_loop(0, MOST, first_conv, 0)
+    ready_weight(0)
+    for r in range(EARLY):
+        first_conv(True, r, 0)
+    lax.fori_loop(EARLY, MOST, functools.partial(first_conv, False), 0)
+    x_start(1, y_finish(1))
     one_way(nx - 1)
-    to_partner(1)
-    x_start(1, y_finish(1))
-    x_start(2, y_finish(2))
+    to_partner(1, 0, nx * size)
+    set_norm(1, x_finish(1), g2[...])
     ready_weight(1)
-    set_norm(1, x_finish(1), g2[...])
 
     my_count = counts[f]
 
     def second_conv(q, r, carry):
+        @pl.when(r >= EARLY)
+        def _():
+            await_bytes(first.at[r, 3], hb_recv.at[r, 0])
+            await_bytes(first.at[r, 0], hb_recv.at[r, 1])
+
         fields = tuple(first.at[r, n] for n in range(4))
         keeps = (keep_top, None, None, keep_bottom)
         result = convolve(r, fields, keeps, q, s2[...], 1)[0] + b2[...]
@@ -495,7 +523,10 @@
         pltpu.make_async_copy(outv.at[r], out.at[r], out_sem.at[r]).start()
         return carry
 
-    lax.fori_loop(0, split, functools.partial(second_conv, 1), 0)
+    lax.fori_loop(0, 1, functools.partial(second_conv, 1), 0)
+    x_start(2, y_finish(2))
+    send_first(MOST - 1)
+    lax.fori_loop(1, split, functools.partial(second_conv, 1), 0)
     set_norm(2, x_finish(2), g2[...])
     lax.fori_loop(split, MOST, functools.partial(second_conv, 2), 0)
 
@@ -516,7 +547,9 @@
         await_bytes(xsc.at[q, 0 : nx - 1], x_send.at[q])
     for r in range(MOST):
         for i in range(2):
-            await_bytes(rec.at[r], ha_send.at[r, i])
+            await_bytes(rec.at[r] if r < EARLY else rec.at[r, i], ha_send.at[r, i])
+            if r >= EARLY:
+                await_bytes(first.at[r, 1 + i], hb_send.at[r, i])
         pltpu.make_async_copy(outv.at[r], out.at[r], out_sem.at[r]).wait()
 
 
@@ -567,7 +600,7 @@
         dma((2,)), dma((8,)), dma((8,)), dma((2,)),
         dma((2,)), dma((2,)), dma((2, 4)), dma((2, 4)), dma((2,)), dma((2,)),
         dma, dma((MOST,)), dma, dma, dma((3,)), dma((3,)), dma((3,)), dma((3,)),
-        dma((MOST, 2)), dma((MOST, 2)), dma((MOST,)), dma((7,)),
+        dma((MOST, 2)), dma((MOST, 2)), dma((MOST, 2)), dma((MOST, 2)), dma((MOST,)), dma((7,)),
         pltpu.SemaphoreType.REGULAR((3, 3)),
     ]
     return pl.pallas_call(

time: 76.1 us -> 72.6 us (0.954)
  the two profiles are of different devices: /device:TPU:128 before, /device:TPU:1 now
where the time goes in v7:
time: 72.6 us; the launch traced here: 72.4 us
  Pallas kernels  70.3 us (97%)
  local copies, waits for them, and re-layouts  2.06 us (3%)
    pallas_call x1, Pallas kernels, per_device(): pl.pallas_call(functools.partial(kernel, nf, nx, ny, frames, su, cells),...  70.3 us
    unnamed x1, local copies, waits for them, and re-layouts  2.06 us

profile of v7, /device:TPU:1, one launch (start us, length us, event | category | flops | bytes accessed | tf_op | source)
XLA Modules:
  0.0 72.4 jit_solution(1783772138586378778)
XLA Ops:
  0.0 70.3 %block.1 = bf16[6,2,128,256]{3,2,1,0:T(8,128)(2,1)} custom-call(s32[16]{0:T(128)} %counts.1, bf16[33,2,8,256]{3,2,1,0:T(8,128)(2,1)} %video.1, bf16[6912,256]{1,0:T(8,128)(2,1)} %tw.1, bf16[9,8,256]{2,1,0:T(8,128)(2,1)} %bitcast.9, bf16[9,8,256]{2,1,0:T(8,128)(2,1)} %bitcast.10, f32[1,256]{1,0:T(1,128)} %bitcast.11, f32[1,256]{1,0:T(1,128)} %bitcast.12, ...), custom_call_target="tpu_custom_call" | custom-call | tf_op jit(solution)/shard_map/block/pallas_call | solution.py:606
  70.3 2.1 %copy.14 = bf16[6,2,128,256]{3,2,1,0:T(8,128)(2,1)} copy(bf16[6,2,128,256]{3,2,1,0:T(8,128)(2,1)} %block.1) | data formatting | bytes 1572864

commit v8 on v5

--- a/solution.py
+++ b/solution.py
@@ -261,7 +261,6 @@
     bordered(0)
     bordered(3)
     lax.fori_loop(0, 3, border_taps, 0)
-    ring(1)
 
     own_w[1].wait()
     for s in range(1, ny):
@@ -388,17 +387,18 @@
         remote(rec.at[r, 0], ha.at[r, 1], ha_send.at[r, 0], ha_recv.at[r, 0], hup, f).start()
         remote(rec.at[r, 1], ha.at[r, 0], ha_send.at[r, 1], ha_recv.at[r, 1], hdn, f).start()
 
-    ring(2)
+    ring(1)
     await_bytes(rs.at[0 : nf - 1], st_recv)
     y_start(0, jnp.sum(rs[...], axis=0))
+    ring(2)
+    slot_in(0)
+    x_start(0, y_finish(0))
     ring(3)
-    slot_in(0)
+    slot_in(1)
+    one_way(0)
+    set_norm(0, x_finish(0), g1[...])
     ring(4)
     to_partner(0)
-    x_start(0, y_finish(0))
-    one_way(0)
-    slot_in(1)
-    set_norm(0, x_finish(0), g1[...])
 
     keeps = (keep_top, None, None, keep_bottom)
 
@@ -440,6 +440,10 @@
     stat[...] = jnp.zeros_like(stat)
     split = MOST - 2
 
+    def send_first(r):
+        remote(first.at[r, 0], hb.at[r, 1], hb_send.at[r, 0], hb_recv.at[r, 0], hup, f).start()
+        remote(first.at[r, 1], hb.at[r, 0], hb_send.at[r, 1], hb_recv.at[r, 1], hdn, f).start()
+
     def sums_start(q):
         y_start(q, hdot(stat[0], sum_map) + hdot(stat[1], sq_map))
 
@@ -471,8 +475,9 @@
         def _():
             sums_start(2)
 
-        remote(first.at[r, 0], hb.at[r, 1], hb_send.at[r, 0], hb_recv.at[r, 0], hup, f).start()
-        remote(first.at[r, 1], hb.at[r, 0], hb_send.at[r, 1], hb_recv.at[r, 1], hdn, f).start()
+        @pl.when(r < MOST - 1)
+        def _():
+            send_first(r)
 
         for n in range(1, nx - 1):
 
@@ -483,12 +488,11 @@
         return carry
 
     lax.fori_loop(0, MOST, first_conv, 0)
+    x_start(1, y_finish(1))
     one_way(nx - 1)
     to_partner(1)
-    x_start(1, y_finish(1))
-    x_start(2, y_finish(2))
+    set_norm(1, x_finish(1), g2[...])
     ready_weight(1)
-    set_norm(1, x_finish(1), g2[...])
 
     my_count = counts[f]
 
@@ -504,7 +508,10 @@
         pltpu.make_async_copy(outv.at[r], out.at[r], out_sem.at[r]).start()
         return carry
 
-    lax.fori_loop(0, split, functools.partial(second_conv, 1), 0)
+    lax.fori_loop(0, 1, functools.partial(second_conv, 1), 0)
+    x_start(2, y_finish(2))
+    send_first(MOST - 1)
+    lax.fori_loop(1, split, functools.partial(second_conv, 1), 0)
     set_norm(2, x_finish(2), g2[...])
     lax.fori_loop(split, MOST, functools.partial(second_conv, 2), 0)
 

time: 68.5 us -> 69.5 us (1.015)
  Pallas kernels: 65.8 us -> 67 us
    pallas_call x1, Pallas kernels: 65.8 us -> 67 us  [per_device(): pl.pallas_call(functools.partial(kernel, nf, nx, ny, frames, su, cells),...]
where the time goes in v8:
time: 69.5 us; the launch traced here: 69 us
  Pallas kernels  67 us (96%)
  local copies, waits for them, and re-layouts  2.06 us (3%)
    pallas_call x1, Pallas kernels, per_device(): pl.pallas_call(functools.partial(kernel, nf, nx, ny, frames, su, cells),...  67 us
    unnamed x1, local copies, waits for them, and re-layouts  2.06 us

profile of v8, /device:TPU:1, one launch (start us, length us, event | category | flops | bytes accessed | tf_op | source)
XLA Modules:
  0.0 69.0 jit_solution(18367728628165311542)
XLA Ops:
  0.0 67.0 %block.1 = bf16[6,2,128,256]{3,2,1,0:T(8,128)(2,1)} custom-call(s32[16]{0:T(128)} %counts.1, bf16[33,2,8,256]{3,2,1,0:T(8,128)(2,1)} %video.1, bf16[6912,256]{1,0:T(8,128)(2,1)} %tw.1, bf16[9,8,256]{2,1,0:T(8,128)(2,1)} %bitcast.9, bf16[9,8,256]{2,1,0:T(8,128)(2,1)} %bitcast.10, f32[1,256]{1,0:T(1,128)} %bitcast.11, f32[1,256]{1,0:T(1,128)} %bitcast.12, ...), custom_call_target="tpu_custom_call" | custom-call | tf_op jit(solution)/shard_map/block/pallas_call | solution.py:590
  67.0 2.1 %copy.14 = bf16[6,2,128,256]{3,2,1,0:T(8,128)(2,1)} copy(bf16[6,2,128,256]{3,2,1,0:T(8,128)(2,1)} %block.1) | data formatting | bytes 1572864
